TPU v7x, 32 devices: a whole 2x2x4 slice. The times are simulated.
32 devices in a mesh: groups: 2 (over y), tile: 4 (over z), vec: 4 (over x, core).
Axes of the slice: x: 2, y: 2, z: 4, core: 2. Of those that a mesh axis runs over, the one named last changes fastest.
Arguments:
- vectors: float32 [2, 256, 3, 8192], P(None, 'vec', None, ('groups', 'tile')), parts along dimension 3, may hold values from -6 to 6
- links: float32 [3, 2, 3, 3, 8192], P(None, None, None, None, ('groups', 'tile')), parts along dimension 4, may hold values from -2.5 to 2.5
- momenta: int32 [8, 3], replicated, may hold values from -2 to 2
- directions: int32 [2], replicated, may hold values from 0 to 5
Outputs:
- elementals: float32 [512, 2, 2, 8, 256], P(('groups', 'tile'), None, None, None, 'vec'), parts along dimension 0
There are 2 independent parts, one for each index of `groups`. A program takes and returns all parts, laid end to end along the dimension named above; an argument that names none is the same for every part. Nothing has to cross between parts.
Inputs may be any that keep to these rules, and one draw needn't show every extreme that they name: directions 0, 1, 2 step forward along the first, second, third dimension; 3, 4, 5 step backward along them.
All inputs are finite; a program needn't handle non-finite values.
Results may differ from a plain program's by a relative error of at most 0.00012.
Values sent between devices are 32-bit elements; how exact they have to be, the bound alone decides.
A program may use at most 128 MiB of HBM per device.

v0:
```python
import math

import jax
import jax.numpy as jnp
from jax import lax
from jax.sharding import PartitionSpec as P

LY = 16
LZ = 32
ITERS = 4


hop_scale = 0.125


def passed_along(value, axis, steps):
    count = lax.axis_size(axis)
    pairs = [(source, (source + steps) % count) for source in range(count)]
    return lax.ppermute(value, axis, pairs)


def extended(x, sides, width):
    for axis, dim in sides:
        count, length = (lax.axis_size(axis), x.shape[dim])
        up = [(i, (i + 1) % count) for i in range(count)]
        down = [(j, i) for i, j in up]
        last = lax.slice_in_dim(x, length - width, length, axis=dim)
        first = lax.slice_in_dim(x, 0, width, axis=dim)
        before = lax.ppermute(last, axis, up)
        after = lax.ppermute(first, axis, down)
        x = jnp.concatenate([before, x, after], axis=dim)
    return x


def link_apply(link_real, link_imag, field_real, field_imag, dagger):
    if dagger:
        link_real = jnp.swapaxes(link_real, 0, 1)
        link_imag = -jnp.swapaxes(link_imag, 0, 1)
    out_real = 0.0
    out_imag = 0.0
    for column in range(3):
        left_real = link_real[:, column][None]
        left_imag = link_imag[:, column][None]
        right_real = field_real[:, column][:, None]
        right_imag = field_imag[:, column][:, None]
        out_real = out_real + left_real * right_real - left_imag * right_imag
        out_imag = out_imag + left_real * right_imag + left_imag * right_real
    return (out_real, out_imag)


def roll_depth(center, step):
    plane_size = center.shape[-1]
    depth_index = jnp.arange(plane_size, dtype=jnp.int32) % LZ
    if step < 0:
        at_edge = depth_index == LZ - 1
        wrapped = jnp.roll(center, LZ - 1, axis=-1)
        plain = jnp.roll(center, -1, axis=-1)
    else:
        at_edge = depth_index == 0
        wrapped = jnp.roll(center, 1 - LZ, axis=-1)
        plain = jnp.roll(center, 1, axis=-1)
    return jnp.where(at_edge, wrapped, plain)


def neighbours(padded):
    center = padded[:, :, :, 1:-1]
    ahead = (padded[:, :, :, 2:], jnp.roll(center, -LZ, axis=4), roll_depth(center, -1))
    behind = (padded[:, :, :, :-2], jnp.roll(center, LZ, axis=4), roll_depth(center, 1))
    return (ahead, behind)


def hop_padded(padded, forward, backward):
    ahead, behind = neighbours(padded)
    total_real = 0.0
    total_imag = 0.0
    for spatial in range(3):
        ahead_real, ahead_imag = link_apply(
            forward[spatial][0], forward[spatial][1], ahead[spatial][0], ahead[spatial][1], False
        )
        behind_real, behind_imag = link_apply(
            backward[spatial][0], backward[spatial][1], behind[spatial][0], behind[spatial][1], True
        )
        total_real = total_real + ahead_real + behind_real
        total_imag = total_imag + ahead_imag + behind_imag
    return hop_scale * jnp.stack([total_real, total_imag])


def phases(momenta, flat_index, extent_x):
    plane_size = LY * LZ
    coord_x = flat_index // plane_size
    coord_y = flat_index % plane_size // LZ
    coord_z = flat_index % LZ
    part_x = jnp.mod(momenta[:, 0:1] * coord_x[None], extent_x).astype(jnp.float32) / extent_x
    part_y = jnp.mod(momenta[:, 1:2] * coord_y[None], LY).astype(jnp.float32) / LY
    part_z = jnp.mod(momenta[:, 2:3] * coord_z[None], LZ).astype(jnp.float32) / LZ
    angle = 2.0 * math.pi * (part_x + part_y + part_z)
    return (jnp.cos(angle), jnp.sin(angle))


def right_matrix(right_stack):
    disp_count = right_stack.shape[0]
    column_count = right_stack.shape[2]
    flat_real = right_stack[:, 0].reshape(disp_count, column_count, -1)
    flat_imag = right_stack[:, 1].reshape(disp_count, column_count, -1)
    real_side = jnp.concatenate([flat_real, flat_imag], axis=2)
    imag_side = jnp.concatenate([flat_imag, -flat_real], axis=2)
    return jnp.stack([real_side, imag_side], axis=1)


def twist_left(left_field, cos_row, sin_row):
    row_count = left_field.shape[1]
    twisted_real = cos_row * left_field[0] - sin_row * left_field[1]
    twisted_imag = cos_row * left_field[1] + sin_row * left_field[0]
    return jnp.concatenate(
        [twisted_real.reshape(row_count, -1), twisted_imag.reshape(row_count, -1)], axis=1
    )


def elemental_each(left_field, right_mat, cosine, sine, norm_factor):

    def one_momentum(phase_pair):
        left_flat = twist_left(left_field, phase_pair[0], phase_pair[1])
        return jnp.einsum("ik,dcjk->idcj", left_flat, right_mat, precision=lax.Precision.HIGHEST)

    result = lax.map(one_momentum, (cosine, sine))
    return jnp.transpose(result, (1, 2, 3, 0, 4)) * norm_factor


def make_shift(link_pair, source, dagger, vector_count, site_count):

    def branch_fn():
        moved = link_apply(link_pair[0], link_pair[1], source[0], source[1], dagger)
        return jnp.stack(moved).reshape(2, vector_count, 3, site_count)

    return branch_fn


def local(vectors, links, momenta, directions):
    nv_dev = vectors.shape[1]
    site_count = vectors.shape[3]
    plane_size = LY * LZ
    plane_count = site_count // plane_size
    tile_count = lax.axis_size("tile")
    disp_count = directions.shape[0]
    extent_x = plane_count * tile_count
    norm_factor = 1.0 / math.sqrt(3.0 * site_count * tile_count)
    gauge = links.reshape(3, 2, 3, 3, plane_count, plane_size)
    last_plane = links[0, :, :, :, site_count - plane_size :]
    rim = passed_along(last_plane, "tile", 1)
    behind_x = jnp.concatenate(
        [rim.reshape(2, 3, 3, 1, plane_size), gauge[0][:, :, :, : plane_count - 1]], axis=3
    )
    forward = [gauge[spatial] for spatial in range(3)]
    backward = [behind_x, jnp.roll(gauge[1], LZ, axis=4), roll_depth(gauge[2], 1)]

    def apply_hop(source):
        padded = extended(source, (("tile", 3),), plane_size)
        padded = padded.reshape(2, nv_dev, 3, plane_count + 2, plane_size)
        return hop_padded(padded, forward, backward).reshape(2, nv_dev, 3, site_count)

    previous = vectors
    current = apply_hop(vectors)
    for order in range(ITERS - 1):
        following = 2.0 * apply_hop(current) - previous
        previous, current = (current, following)
    padded_field = extended(current, (("tile", 3),), plane_size)
    padded_field = padded_field.reshape(2, nv_dev, 3, plane_count + 2, plane_size)
    ahead, behind = neighbours(padded_field)
    branches = [
        make_shift(forward[heading], ahead[heading], False, nv_dev, site_count)
        for heading in range(3)
    ]
    branches = branches + [
        make_shift(backward[heading], behind[heading], True, nv_dev, site_count)
        for heading in range(3)
    ]
    displaced = jnp.stack(
        [lax.switch(directions[disp_slot], branches) for disp_slot in range(disp_count)]
    )
    flat_index = lax.axis_index("tile") * site_count + jnp.arange(site_count, dtype=jnp.int32)
    cosine, sine = phases(momenta, flat_index, extent_x)
    right_mat = right_matrix(displaced)
    partial_rows = elemental_each(
        lax.all_gather(current, "vec", axis=1, tiled=True), right_mat, cosine, sine, norm_factor
    )
    return lax.psum_scatter(partial_rows, "tile", scatter_dimension=0, tiled=True)


def solution(mesh):
    return jax.shard_map(
        local,
        mesh=mesh,
        in_specs=(
            P(None, "vec", None, ("groups", "tile")),
            P(None, None, None, None, ("groups", "tile")),
            P(),
            P(),
        ),
        out_specs=P(("groups", "tile"), None, None, None, "vec"),
        check_vma=False,
    )
```

profile of v0, /device:TPU:0, one launch (start us, length us, event | category | flops | bytes accessed | tf_op | source)
XLA Modules:
  0.0 778.7 jit_solution(13172530853241620579)
XLA Ops:
  20.9 28.8 %collective-permute-done.2 = f32[2,3,3,512]{3,0,2,1:T(2,128)S(1)} collective-permute-done((f32[2,3,3,512]{3,0,2,1:T(2,128)S(1)}, f32[2,3,3,512]{3,0,2,1:T(2,128)S(1)}, u32[]{:S(2)}, u32[]{:S(2)}) %collective-permute-start.2) | collective-permute-done | bytes 36896 | tf_op jit(solution)/shard_map/ppermute | solution.py:19
  100.7 18.4 %collective-permute-done.3 = f32[2,64,3,512]{3,1,2,0:T(8,128)S(1)} collective-permute-done((f32[2,64,3,512]{3,1,2,0:T(8,128)S(1)}, f32[2,64,3,512]{3,1,2,0:T(8,128)S(1)}, u32[]{:S(2)}, u32[]{:S(2)}) %collective-permute-start.3) | collective-permute-done | bytes 786464 | tf_op jit(solution)/shard_map/ppermute | solution.py:29
  119.1 13.1 %collective-permute-done.4 = f32[2,64,3,512]{3,1,2,0:T(8,128)S(1)} collective-permute-done((f32[2,64,3,512]{3,1,2,0:T(8,128)S(1)}, f32[2,64,3,512]{3,1,2,0:T(8,128)S(1)}, u32[]{:S(2)}, u32[]{:S(2)}) %collective-permute-start.4) | collective-permute-done | bytes 786464 | tf_op jit(solution)/shard_map/ppermute | solution.py:30
  179.1 18.4 %collective-permute-done.5 = f32[2,64,3,512]{3,1,2,0:T(8,128)S(1)} collective-permute-done((f32[2,64,3,512]{3,1,2,0:T(8,128)S(1)}, f32[2,64,3,512]{3,1,2,0:T(8,128)S(1)}, u32[]{:S(2)}, u32[]{:S(2)}) %collective-permute-start.5) | collective-permute-done | bytes 786464 | tf_op jit(solution)/shard_map/ppermute | solution.py:29
  197.4 13.1 %collective-permute-done.6 = f32[2,64,3,512]{3,1,2,0:T(8,128)S(1)} collective-permute-done((f32[2,64,3,512]{3,1,2,0:T(8,128)S(1)}, f32[2,64,3,512]{3,1,2,0:T(8,128)S(1)}, u32[]{:S(2)}, u32[]{:S(2)}) %collective-permute-start.6) | collective-permute-done | bytes 786464 | tf_op jit(solution)/shard_map/ppermute | solution.py:30
  256.8 18.4 %collective-permute-done.7 = f32[2,64,3,512]{3,1,2,0:T(8,128)S(1)} collective-permute-done((f32[2,64,3,512]{3,1,2,0:T(8,128)S(1)}, f32[2,64,3,512]{3,1,2,0:T(8,128)S(1)}, u32[]{:S(2)}, u32[]{:S(2)}) %collective-permute-start.7) | collective-permute-done | bytes 786464 | tf_op jit(solution)/shard_map/ppermute | solution.py:29
  275.2 14.9 %collective-permute-done.8 = f32[2,64,3,512]{3,1,2,0:T(8,128)S(1)} collective-permute-done((f32[2,64,3,512]{3,1,2,0:T(8,128)S(1)}, f32[2,64,3,512]{3,1,2,0:T(8,128)S(1)}, u32[]{:S(2)}, u32[]{:S(2)}) %collective-permute-start.8) | collective-permute-done | bytes 786464 | tf_op jit(solution)/shard_map/ppermute | solution.py:30
  342.1 17.4 %collective-permute-done.10 = f32[2,64,3,512]{3,1,2,0:T(8,128)S(1)} collective-permute-done((f32[2,64,3,512]{3,1,2,0:T(8,128)S(1)}, f32[2,64,3,512]{3,1,2,0:T(8,128)S(1)}, u32[]{:S(2)}, u32[]{:S(2)}) %collective-permute-start.10) | collective-permute-done | bytes 786464 | tf_op jit(solution)/shard_map/ppermute | solution.py:30
  359.5 15.4 %collective-permute-done.9 = f32[2,64,3,512]{3,1,2,0:T(8,128)S(1)} collective-permute-done((f32[2,64,3,512]{3,1,2,0:T(8,128)S(1)}, f32[2,64,3,512]{3,1,2,0:T(8,128)S(1)}, u32[]{:S(2)}, u32[]{:S(2)}) %collective-permute-start.9) | collective-permute-done | bytes 786464 | tf_op jit(solution)/shard_map/ppermute | solution.py:29
  406.3 14.1 %conditional.2 = (f32[1,2,64,3,1024]{4,3,2,1,0:T(4,128)}) conditional(s32[]{:T(128)} %bitcast.162, (f32[2,3,3,2,512]{4,3,0,2,1:T(2,128)S(1)}, f32[2,64,3,2,512]{4,3,1,2,0:T(2,128)S(1)}) %tuple.597, (f32[2,3,3,2,512]{4,3,0,2,1:T(2,128)S(1)}, f32[2,64,3,2,512]{4,3,1,2,0:T(2,128)S(1)}) %tuple.593, ...), branch_computations={%region_0.1_spmd, %region_1.2_spmd, %region_2.3_spmd, %region_3.4_... | conditional | flops 4727808 | bytes 16539684 | solution.py:178
  420.4 14.8 %conditional.3 = (f32[1,2,64,3,1024]{4,3,2,1,0:T(4,128)S(1)}) conditional(s32[]{:T(128)} %bitcast.163, (f32[2,3,3,2,512]{4,3,0,2,1:T(2,128)S(1)}, f32[2,64,3,2,512]{4,3,1,2,0:T(2,128)}) %tuple.598, (f32[2,3,3,2,512]{4,3,0,2,1:T(2,128)S(1)}, f32[2,64,3,2,512]{4,3,1,2,0:T(2,128)S(1)}) %tuple.594, ...), branch_computations={%region_6.7_spmd, %region_7.8_spmd, %region_8.9_spmd, %region_9.10... | conditional | flops 4727808 | bytes 16539684 | solution.py:178
  452.1 10.2 %copy.471 = f32[2,256,3,1024]{1,3,2,0:T(8,128)} copy(f32[2,256,3,1024]{3,0,2,1:T(2,128)} %all-gather.2.cloned.1.call-done) | data formatting | bytes 12582912 | tf_op jit(solution)/shard_map/while | solution.py:125
  462.2 250.6 %while.10 = (s32[]{:T(128)}, f32[8,256,2,2,64]{1,4,3,2,0:T(8,128)}, f32[8,1024]{1,0:T(8,128)}, f32[2,256,3,1024]{1,3,2,0:T(8,128)}, f32[8,1024]{1,0:T(8,128)S(1)}, /*index=5*/f32[2,2,64,6144]{3,2,1,0:T(8,128)}, s32[]{:T(128)}) while((s32[]{:T(128)}, f32[8,256,2,2,64]{1,4,3,2,0:T(8,128)}, f32[8,1024]{1,0:T(8,128)}, ...), condition=%wide.region_13.14_spmd, body=%wide.region_12.13_spmd.sunk | while | flops 4838129664 | bytes 50717264 | solution.py:125
  478.3 15.3 %fusion.221 = f32[8,256,2,2,64]{1,4,3,2,0:T(8,128)} fusion(f32[8,256,2,2,64]{1,4,3,2,0:T(8,128)} %get-tuple-element.986, s32[]{:T(128)} %get-tuple-element.985, f32[2,2,64,6144]{3,2,1,0:T(8,128)} %get-tuple-element.997, f32[256,3072]{1,0:T(8,128)S(1)} %get-tuple-element.976, f32[256,3072]{1,0:T(8,128)S(1)} %get-tuple-element.977), kind=kOutput, calls=%fused_computation.167.clone.1 | convolution fusion | flops 4833411072 | bytes 12845568 | tf_op jit(solution)/shard_map/while/body/eval_jaxpr/ik,dcjk->idcj/dot_general | solution.py:123
  509.6 15.3 %fusion.221 = f32[8,256,2,2,64]{1,4,3,2,0:T(8,128)} fusion(f32[8,256,2,2,64]{1,4,3,2,0:T(8,128)} %get-tuple-element.986, s32[]{:T(128)} %get-tuple-element.985, f32[2,2,64,6144]{3,2,1,0:T(8,128)} %get-tuple-element.997, f32[256,3072]{1,0:T(8,128)S(1)} %get-tuple-element.976, f32[256,3072]{1,0:T(8,128)S(1)} %get-tuple-element.977), kind=kOutput, calls=%fused_computation.167.clone.1 | convolution fusion | flops 4833411072 | bytes 12845568 | tf_op jit(solution)/shard_map/while/body/eval_jaxpr/ik,dcjk->idcj/dot_general | solution.py:123
  541.0 15.3 %fusion.221 = f32[8,256,2,2,64]{1,4,3,2,0:T(8,128)} fusion(f32[8,256,2,2,64]{1,4,3,2,0:T(8,128)} %get-tuple-element.986, s32[]{:T(128)} %get-tuple-element.985, f32[2,2,64,6144]{3,2,1,0:T(8,128)} %get-tuple-element.997, f32[256,3072]{1,0:T(8,128)S(1)} %get-tuple-element.976, f32[256,3072]{1,0:T(8,128)S(1)} %get-tuple-element.977), kind=kOutput, calls=%fused_computation.167.clone.1 | convolution fusion | flops 4833411072 | bytes 12845568 | tf_op jit(solution)/shard_map/while/body/eval_jaxpr/ik,dcjk->idcj/dot_general | solution.py:123
  572.3 15.3 %fusion.221 = f32[8,256,2,2,64]{1,4,3,2,0:T(8,128)} fusion(f32[8,256,2,2,64]{1,4,3,2,0:T(8,128)} %get-tuple-element.986, s32[]{:T(128)} %get-tuple-element.985, f32[2,2,64,6144]{3,2,1,0:T(8,128)} %get-tuple-element.997, f32[256,3072]{1,0:T(8,128)S(1)} %get-tuple-element.976, f32[256,3072]{1,0:T(8,128)S(1)} %get-tuple-element.977), kind=kOutput, calls=%fused_computation.167.clone.1 | convolution fusion | flops 4833411072 | bytes 12845568 | tf_op jit(solution)/shard_map/while/body/eval_jaxpr/ik,dcjk->idcj/dot_general | solution.py:123
  603.6 15.3 %fusion.221 = f32[8,256,2,2,64]{1,4,3,2,0:T(8,128)} fusion(f32[8,256,2,2,64]{1,4,3,2,0:T(8,128)} %get-tuple-element.986, s32[]{:T(128)} %get-tuple-element.985, f32[2,2,64,6144]{3,2,1,0:T(8,128)} %get-tuple-element.997, f32[256,3072]{1,0:T(8,128)S(1)} %get-tuple-element.976, f32[256,3072]{1,0:T(8,128)S(1)} %get-tuple-element.977), kind=kOutput, calls=%fused_computation.167.clone.1 | convolution fusion | flops 4833411072 | bytes 12845568 | tf_op jit(solution)/shard_map/while/body/eval_jaxpr/ik,dcjk->idcj/dot_general | solution.py:123
  619.7 6.4 fusion.220
  635.0 15.3 %fusion.221 = f32[8,256,2,2,64]{1,4,3,2,0:T(8,128)} fusion(f32[8,256,2,2,64]{1,4,3,2,0:T(8,128)} %get-tuple-element.986, s32[]{:T(128)} %get-tuple-element.985, f32[2,2,64,6144]{3,2,1,0:T(8,128)} %get-tuple-element.997, f32[256,3072]{1,0:T(8,128)S(1)} %get-tuple-element.976, f32[256,3072]{1,0:T(8,128)S(1)} %get-tuple-element.977), kind=kOutput, calls=%fused_computation.167.clone.1 | convolution fusion | flops 4833411072 | bytes 12845568 | tf_op jit(solution)/shard_map/while/body/eval_jaxpr/ik,dcjk->idcj/dot_general | solution.py:123
  666.3 15.3 %fusion.221 = f32[8,256,2,2,64]{1,4,3,2,0:T(8,128)} fusion(f32[8,256,2,2,64]{1,4,3,2,0:T(8,128)} %get-tuple-element.986, s32[]{:T(128)} %get-tuple-element.985, f32[2,2,64,6144]{3,2,1,0:T(8,128)} %get-tuple-element.997, f32[256,3072]{1,0:T(8,128)S(1)} %get-tuple-element.976, f32[256,3072]{1,0:T(8,128)S(1)} %get-tuple-element.977), kind=kOutput, calls=%fused_computation.167.clone.1 | convolution fusion | flops 4833411072 | bytes 12845568 | tf_op jit(solution)/shard_map/while/body/eval_jaxpr/ik,dcjk->idcj/dot_general | solution.py:123
  697.6 15.3 %fusion.221 = f32[8,256,2,2,64]{1,4,3,2,0:T(8,128)} fusion(f32[8,256,2,2,64]{1,4,3,2,0:T(8,128)} %get-tuple-element.986, s32[]{:T(128)} %get-tuple-element.985, f32[2,2,64,6144]{3,2,1,0:T(8,128)} %get-tuple-element.997, f32[256,3072]{1,0:T(8,128)S(1)} %get-tuple-element.976, f32[256,3072]{1,0:T(8,128)S(1)} %get-tuple-element.977), kind=kOutput, calls=%fused_computation.167.clone.1 | convolution fusion | flops 4833411072 | bytes 12845568 | tf_op jit(solution)/shard_map/while/body/eval_jaxpr/ik,dcjk->idcj/dot_general | solution.py:123
  719.2 6.7 reshape.4513
  725.9 42.8 %reduce-scatter.4.cloned.1.call-done = f32[64,2048]{1,0:T(8,128)} async-done(((f32[256,2048]{1,0:T(8,128)}), f32[64,2048]{1,0:T(8,128)}) %reduce-scatter.4.cloned.1.call-update) | async-done | bytes 524304
  (659 shorter events, 395.5 us)
Async XLA Ops:
  6.5 7.8 copy-start.65
  6.5 445.6 %all-gather.2.cloned.1.call-start = ((), (), s32[]{:S(2)}) async-start(), calls=%async_computation.1 | async-start | bytes 7864320 | tf_op jit(solution)/shard_map/all_gather | solution.py:184
  9.2 44.3 %collective-permute-start = (f32[2,64,3,512]{3,1,2,0:T(8,128)}, f32[2,64,3,512]{3,1,2,0:T(8,128)S(1)}, u32[]{:S(2)}, u32[]{:S(2)}) collective-permute-start(f32[2,64,3,512]{3,1,2,0:T(8,128)} %get-tuple-element.710), channel_id=1, source_target_pairs={{0,4},{4,8},{8,12},{12,0},{1,5},{5,9},{9,13},{13,1},{2,6},{6,10},{... | collective-permute-start | bytes 2359304 | tf_op jit(solution)/shard_map/ppermute | solution.py:29
  12.3 41.2 %collective-permute-start.1 = (f32[2,64,3,512]{3,1,2,0:T(8,128)}, f32[2,64,3,512]{3,1,2,0:T(8,128)}, u32[]{:S(2)}, u32[]{:S(2)}) collective-permute-start(f32[2,64,3,512]{3,1,2,0:T(8,128)} %get-tuple-element.711), channel_id=1, source_target_pairs={{4,0},{8,4},{12,8},{0,12},{5,1},{9,5},{13,9},{1,13},{6,2},{10,6},{... | collective-permute-start | bytes 2359304 | tf_op jit(solution)/shard_map/ppermute | solution.py:30
  14.3 35.4 %collective-permute-start.2 = (f32[2,3,3,512]{3,0,2,1:T(2,128)S(1)}, f32[2,3,3,512]{3,0,2,1:T(2,128)S(1)}, u32[]{:S(2)}, u32[]{:S(2)}) collective-permute-start(f32[2,3,3,512]{3,0,2,1:T(2,128)S(1)} %slice_bitcast_fusion.147), channel_id=1, source_target_pairs={{0,4},{4,8},{8,12},{12,0},{1,5},{5,9},{9,13},{13,1},{2,6},{6,10},{... | collective-permute-start | bytes 110600 | tf_op jit(solution)/shard_map/ppermute | solution.py:19
  16.2 37.3 %copy-start.15 = (f32[2,3,3,2,512]{4,3,0,2,1:T(2,128)}, f32[2,3,3,2,512]{4,3,0,2,1:T(2,128)S(1)}, u32[]{:S(2)}) copy-start(f32[2,3,3,2,512]{4,3,0,2,1:T(2,128)S(1)} %squeeze.345) | copy-start | bytes 221188
  16.2 37.3 %copy-start = (f32[2,64,3,1024]{3,1,2,0:T(8,128)S(1)}, f32[2,64,3,1024]{3,1,2,0:T(8,128)}, u32[]{:S(2)}) copy-start(f32[2,64,3,1024]{3,1,2,0:T(8,128)} %param.18) | copy-start | bytes 4718596
  17.7 35.8 %copy-start.63 = (f32[2,3,3,2,512]{4,3,0,2,1:T(2,128)}, f32[2,3,3,2,512]{4,3,0,2,1:T(2,128)S(1)}, u32[]{:S(2)}) copy-start(f32[2,3,3,2,512]{4,3,0,2,1:T(2,128)S(1)} %squeeze.327) | copy-start | bytes 221188
  49.8 3.8 copy-start.68
  96.9 22.3 %collective-permute-start.3 = (f32[2,64,3,512]{3,1,2,0:T(8,128)S(1)}, f32[2,64,3,512]{3,1,2,0:T(8,128)S(1)}, u32[]{:S(2)}, u32[]{:S(2)}) collective-permute-start(f32[2,64,3,512]{3,1,2,0:T(8,128)S(1)} %get-tuple-element.704), channel_id=1, source_target_pairs={{0,4},{4,8},{8,12},{12,0},{1,5},{5,9},{9,13},{13,1},{2,6},{6,10},{... | collective-permute-start | bytes 2359304 | tf_op jit(solution)/shard_map/ppermute | solution.py:29
  96.9 35.3 %collective-permute-start.4 = (f32[2,64,3,512]{3,1,2,0:T(8,128)S(1)}, f32[2,64,3,512]{3,1,2,0:T(8,128)S(1)}, u32[]{:S(2)}, u32[]{:S(2)}) collective-permute-start(f32[2,64,3,512]{3,1,2,0:T(8,128)S(1)} %get-tuple-element.705), channel_id=1, source_target_pairs={{4,0},{8,4},{12,8},{0,12},{5,1},{9,5},{13,9},{1,13},{6,2},{10,6},{... | collective-permute-start | bytes 2359304 | tf_op jit(solution)/shard_map/ppermute | solution.py:30
  175.2 22.3 %collective-permute-start.5 = (f32[2,64,3,512]{3,1,2,0:T(8,128)S(1)}, f32[2,64,3,512]{3,1,2,0:T(8,128)S(1)}, u32[]{:S(2)}, u32[]{:S(2)}) collective-permute-start(f32[2,64,3,512]{3,1,2,0:T(8,128)S(1)} %get-tuple-element.698), channel_id=1, source_target_pairs={{0,4},{4,8},{8,12},{12,0},{1,5},{5,9},{9,13},{13,1},{2,6},{6,10},{... | collective-permute-start | bytes 2359304 | tf_op jit(solution)/shard_map/ppermute | solution.py:29
  175.2 35.3 %collective-permute-start.6 = (f32[2,64,3,512]{3,1,2,0:T(8,128)S(1)}, f32[2,64,3,512]{3,1,2,0:T(8,128)S(1)}, u32[]{:S(2)}, u32[]{:S(2)}) collective-permute-start(f32[2,64,3,512]{3,1,2,0:T(8,128)S(1)} %get-tuple-element.699), channel_id=1, source_target_pairs={{4,0},{8,4},{12,8},{0,12},{5,1},{9,5},{13,9},{1,13},{6,2},{10,6},{... | collective-permute-start | bytes 2359304 | tf_op jit(solution)/shard_map/ppermute | solution.py:30
  252.9 22.3 %collective-permute-start.7 = (f32[2,64,3,512]{3,1,2,0:T(8,128)S(1)}, f32[2,64,3,512]{3,1,2,0:T(8,128)S(1)}, u32[]{:S(2)}, u32[]{:S(2)}) collective-permute-start(f32[2,64,3,512]{3,1,2,0:T(8,128)S(1)} %get-tuple-element.692), channel_id=1, source_target_pairs={{0,4},{4,8},{8,12},{12,0},{1,5},{5,9},{9,13},{13,1},{2,6},{6,10},{... | collective-permute-start | bytes 2359304 | tf_op jit(solution)/shard_map/ppermute | solution.py:29
  254.5 35.5 %collective-permute-start.8 = (f32[2,64,3,512]{3,1,2,0:T(8,128)S(1)}, f32[2,64,3,512]{3,1,2,0:T(8,128)S(1)}, u32[]{:S(2)}, u32[]{:S(2)}) collective-permute-start(f32[2,64,3,512]{3,1,2,0:T(8,128)S(1)} %get-tuple-element.693), channel_id=1, source_target_pairs={{4,0},{8,4},{12,8},{0,12},{5,1},{9,5},{13,9},{1,13},{6,2},{10,6},{... | collective-permute-start | bytes 2359304 | tf_op jit(solution)/shard_map/ppermute | solution.py:30
  328.5 3.4 copy-start.2
  328.5 3.4 copy-start.6
  328.5 3.4 copy-start.8
  335.0 433.7 %reduce-scatter.4.cloned.1.call-start = ((), (), s32[]{:S(2)}) async-start(), calls=%async_computation.2 | async-start | bytes 2621440
  338.3 3.7 copy-start.64
  338.3 3.7 copy-start.69
  338.5 21.0 %collective-permute-start.10 = (f32[2,64,3,512]{3,1,2,0:T(8,128)S(1)}, f32[2,64,3,512]{3,1,2,0:T(8,128)S(1)}, u32[]{:S(2)}, u32[]{:S(2)}) collective-permute-start(f32[2,64,3,512]{3,1,2,0:T(8,128)S(1)} %get-tuple-element.687), channel_id=1, source_target_pairs={{4,0},{8,4},{12,8},{0,12},{5,1},{9,5},{13,9},{1,13},{6,2},{10,6},{... | collective-permute-start | bytes 2359304 | tf_op jit(solution)/shard_map/ppermute | solution.py:30
  341.2 33.7 %collective-permute-start.9 = (f32[2,64,3,512]{3,1,2,0:T(8,128)S(1)}, f32[2,64,3,512]{3,1,2,0:T(8,128)S(1)}, u32[]{:S(2)}, u32[]{:S(2)}) collective-permute-start(f32[2,64,3,512]{3,1,2,0:T(8,128)S(1)} %get-tuple-element.686), channel_id=1, source_target_pairs={{0,4},{4,8},{8,12},{12,0},{1,5},{5,9},{9,13},{13,1},{2,6},{6,10},{... | collective-permute-start | bytes 2359304 | tf_op jit(solution)/shard_map/ppermute | solution.py:29
  388.5 3.8 copy-start.82
  (73 other events, 83.9 us)
Sparse Core Ops, SparseCore 0:
  335.1 46.2 all-gather.1
  726.0 42.6 reduce-scatter.3
where the time goes:
time: 785 us; the launch traced here: 779 us
  local copies, waits for them, and re-layouts  274 us (35%)
  waiting for transfers between devices  201 us (26%)
  other arithmetic  126 us (16%)
  matrix products  122 us (16%)
  starting transfers between devices  19.4 us (2%)
  loops' own time  18.9 us (2%)
  between operations  18.2 us (2%)
    dot_general x8, matrix products, one_momentum(): jnp.einsum('ik,dcjk->idcj', left_flat, right_mat, precision=lax.Precision...  122 us
    ppermute x5, waiting for transfers between devices, extended(): before = lax.ppermute(last, axis, up)  70.6 us
    ppermute x5, waiting for transfers between devices, extended(): after = lax.ppermute(first, axis, down)  58.5 us
    slice x8, local copies, waits for them, and re-layouts, twist_left(): twisted_real = cos_row * left_field[0] - sin_row * left_field[1]  51.1 us
    squeeze x16, local copies, waits for them, and re-layouts, twist_left(): twisted_real = cos_row * left_field[0] - sin_row * left_field[1]  48.1 us
    unnamed x3, waiting for transfers between devices  42.8 us
    unnamed x358, local copies, waits for them, and re-layouts  34.1 us
    select_n x10, other arithmetic, roll_depth(): return jnp.where(at_edge, wrapped, plain)  31.6 us
  transfers between devices with their start and end apart: 13, of which 10 were waited for; matrix products, arithmetic and copies ran while one was open for 9% of the time, Pallas kernels for 0%

commit v1 on v0

v1 whole, which is shorter than its diff:
```python
import functools
import math

import jax
import jax.numpy as jnp
from jax import lax
from jax.experimental import pallas as pl
from jax.experimental.pallas import tpu as pltpu
from jax.sharding import PartitionSpec as P

LY = 16
LZ = 32
ITERS = 4
PLANE = LY * LZ
LANES = 128
PER_PLANE = PLANE // LANES
HOP_SCALE = 0.125
VMEM_LIMIT = 60 * 1024 * 1024


def lane_index(like):
    return lax.broadcasted_iota(jnp.int32, like.shape, len(like.shape) - 1)


def shift_z(value, step):
    axis = len(value.shape) - 1
    lane = lane_index(value) % LZ
    if step > 0:
        plain = pltpu.roll(value, LANES - 1, axis)
        wrapped = pltpu.roll(value, LZ - 1, axis)
        return jnp.where(lane == LZ - 1, wrapped, plain)
    plain = pltpu.roll(value, 1, axis)
    wrapped = pltpu.roll(value, LANES - LZ + 1, axis)
    return jnp.where(lane == 0, wrapped, plain)


def shift_y(value, other, step):
    axis = len(value.shape) - 1
    lane = lane_index(value)
    if step > 0:
        return pltpu.roll(jnp.where(lane < LZ, other, value), LANES - LZ, axis)
    return pltpu.roll(jnp.where(lane >= LANES - LZ, other, value), LZ, axis)


def in_plane(chunk, step):
    base = chunk // PER_PLANE * PER_PLANE
    return base + (chunk + step + PER_PLANE) % PER_PLANE


def link_row(links, chunk, spatial, part, row, column):
    index = (part * 3 + row) * 3 + column
    return links[chunk, spatial, index : index + 1, :]


def apply_link(links, chunk, spatial, dagger, field, total):
    for row in range(3):
        real, imag = total[row], total[3 + row]
        for column in range(3):
            a, b = (column, row) if dagger else (row, column)
            lr = link_row(links, chunk, spatial, 0, a, b)
            li = link_row(links, chunk, spatial, 1, a, b)
            vr, vi = field[column], field[3 + column]
            if dagger:
                dr = lr * vr + li * vi
                di = lr * vi - li * vr
            else:
                dr = lr * vr - li * vi
                di = lr * vi + li * vr
            real = dr if real is None else real + dr
            imag = di if imag is None else imag + di
        total[row], total[3 + row] = real, imag
    return total


def moved(read, chunk, spatial, step, ahead_x):
    if spatial == 0:
        return [read(ahead_x, comp) for comp in range(6)]
    if spatial == 1:
        other = in_plane(chunk, step)
        return [shift_y(read(chunk, comp), read(other, comp), step) for comp in range(6)]
    return [shift_z(read(chunk, comp), step) for comp in range(6)]


def filter_kernel(field_ref, links_ref, out_ref, back_ref, first, second):
    chunks = field_ref.shape[0]

    @pl.loop(0, chunks)
    def _(chunk):
        back_ref[chunk, 0] = links_ref[(chunk - PER_PLANE + chunks) % chunks, 0]
        back_ref[chunk, 1] = shift_y(
            links_ref[chunk, 1], links_ref[in_plane(chunk, -1), 1], -1
        )
        back_ref[chunk, 2] = shift_z(links_ref[chunk, 2], -1)

    def hop(source, previous, target):
        @pl.loop(0, chunks)
        def _(chunk):
            read = lambda at, comp: source[at, comp]
            total = [None] * 6
            for spatial in range(3):
                ahead = moved(read, chunk, spatial, 1, (chunk + PER_PLANE) % chunks)
                total = apply_link(links_ref, chunk, spatial, False, ahead, total)
                behind = moved(
                    read, chunk, spatial, -1, (chunk - PER_PLANE + chunks) % chunks
                )
                total = apply_link(back_ref, chunk, spatial, True, behind, total)
            for comp in range(6):
                if previous is None:
                    target[chunk, comp] = HOP_SCALE * total[comp]
                else:
                    target[chunk, comp] = (
                        2.0 * HOP_SCALE * total[comp] - previous[chunk, comp]
                    )

    hop(field_ref, None, first)
    older, newer = field_ref, first
    for order in range(ITERS - 1):
        target = out_ref if order == ITERS - 2 else (second if order % 2 == 0 else first)
        hop(newer, older, target)
        older, newer = newer, target


def split(value):
    high = value.astype(jnp.bfloat16)
    low = (value - high.astype(jnp.float32)).astype(jnp.bfloat16)
    return high, low


def contract_kernel(
    dirs_ref, rows_ref, cols_ref, links_ref, back_ref, cos_ref, sin_ref,
    out_ref, shifted, left_hi, left_lo, right_hi, right_lo,
):
    chunk = pl.program_id(0)
    disps = shifted.shape[0]
    columns = cols_ref.shape[2]
    row_count = rows_ref.shape[2]
    momenta = cos_ref.shape[1]
    read = lambda at, comp: cols_ref[at + PER_PLANE, comp]

    for disp in range(disps):
        for heading in range(6):
            @pl.when(dirs_ref[disp] == heading)
            def _(disp=disp, heading=heading):
                spatial = heading % 3
                step = 1 if heading < 3 else -1
                for block in range(0, columns, 16):
                    stop = min(columns, block + 16)
                    part = lambda at, comp: cols_ref[at + PER_PLANE, comp, block:stop, :]
                    source = moved(part, chunk, spatial, step, chunk + step * PER_PLANE)
                    table = links_ref if step > 0 else back_ref
                    total = apply_link(table, chunk, spatial, step < 0, source, [None] * 6)
                    for comp in range(6):
                        shifted[disp, comp, block:stop, :] = total[comp]

    for colour in range(3):
        real_at = pl.ds(2 * colour * LANES, LANES)
        imag_at = pl.ds((2 * colour + 1) * LANES, LANES)
        hi, lo = split(rows_ref[0, colour])
        hi_i, lo_i = split(rows_ref[0, 3 + colour])
        for half, store_r, store_i in ((left_hi, hi, hi_i), (left_lo, lo, lo_i)):
            half[0:row_count, real_at] = store_r
            half[0:row_count, imag_at] = store_i
            half[row_count : 2 * row_count, real_at] = -store_i
            half[row_count : 2 * row_count, imag_at] = store_r
        for disp in range(disps):
            dr = shifted[disp, colour]
            di = shifted[disp, 3 + colour]
            for p in range(momenta):
                c = cos_ref[0, p : p + 1, :]
                s = sin_ref[0, p : p + 1, :]
                at = pl.ds((p * disps + disp) * columns, columns)
                hi, lo = split(c * dr + s * di)
                right_hi[at, real_at] = hi
                right_lo[at, real_at] = lo
                hi, lo = split(c * di - s * dr)
                right_hi[at, imag_at] = hi
                right_lo[at, imag_at] = lo

    @pl.when(chunk == 0)
    def _():
        out_ref[...] = jnp.zeros_like(out_ref)

    dims = (((1,), (1,)), ((), ()))
    dot = functools.partial(
        lax.dot_general, dimension_numbers=dims, preferred_element_type=jnp.float32
    )
    width = min(256, right_hi.shape[0])

    @pl.loop(0, right_hi.shape[0] // width)
    def _(block):
        at = pl.ds(pl.multiple_of(block * width, width), width)
        rh, rl = right_hi[at, :], right_lo[at, :]
        out_ref[:, at] += (
            dot(left_hi[...], rl) + dot(left_lo[...], rh) + dot(left_hi[...], rh)
        )


def phases(momenta, flat_index, extent_x):
    coord_x = flat_index // PLANE
    coord_y = flat_index % PLANE // LZ
    coord_z = flat_index % LZ
    part_x = jnp.mod(momenta[:, 0:1] * coord_x[None], extent_x).astype(jnp.float32) / extent_x
    part_y = jnp.mod(momenta[:, 1:2] * coord_y[None], LY).astype(jnp.float32) / LY
    part_z = jnp.mod(momenta[:, 2:3] * coord_z[None], LZ).astype(jnp.float32) / LZ
    angle = 2.0 * math.pi * (part_x + part_y + part_z)
    return (jnp.cos(angle), jnp.sin(angle))


def local(vectors, links, momenta, directions):
    nv = vectors.shape[1]
    sites = vectors.shape[3]
    tiles = lax.axis_size("tile")
    disps = directions.shape[0]
    moms = momenta.shape[0]
    chunks = sites // LANES
    every = chunks * tiles
    share = nv // tiles
    norm = 1.0 / math.sqrt(3.0 * sites * tiles)
    me = lax.axis_index("tile")

    field = vectors.reshape(2, tiles, share, 3, chunks, LANES)
    field = field.transpose(1, 4, 0, 3, 2, 5).reshape(tiles, chunks, 6, share, LANES)
    field = lax.all_to_all(field, "tile", 0, 0)
    field = field.reshape(every, 6, share, LANES)
    own_links = links.reshape(3, 18, chunks, LANES).transpose(2, 0, 1, 3)
    all_links = lax.all_gather(own_links, "tile", axis=0, tiled=True)

    vmem = pl.BlockSpec(memory_space=pltpu.VMEM)
    filtered, back = pl.pallas_call(
        filter_kernel,
        out_shape=(
            jax.ShapeDtypeStruct(field.shape, jnp.float32),
            jax.ShapeDtypeStruct(all_links.shape, jnp.float32),
        ),
        in_specs=[vmem, vmem],
        out_specs=(vmem, vmem),
        scratch_shapes=[pltpu.VMEM(field.shape, jnp.float32)] * 2,
        compiler_params=pltpu.CompilerParams(vmem_limit_bytes=VMEM_LIMIT),
        name="filter",
    )(field, all_links)

    slabs = filtered.reshape(tiles, chunks, 6, share, LANES)
    before = jnp.roll(slabs[:, chunks - PER_PLANE :], 1, axis=0)
    after = jnp.roll(slabs[:, :PER_PLANE], -1, axis=0)
    slabs = jnp.concatenate([before, slabs, after], axis=1)
    slabs = lax.all_to_all(slabs, "tile", 0, 0)
    wide = chunks + 2 * PER_PLANE
    cols = slabs.transpose(1, 2, 0, 3, 4).reshape(wide, 6, nv, LANES)
    rows = lax.all_gather(
        cols[PER_PLANE : PER_PLANE + chunks], "vec", axis=2, tiled=True
    )
    row_count = rows.shape[2]
    own_back = lax.dynamic_slice_in_dim(back, me * chunks, chunks, 0)

    flat_index = me * sites + jnp.arange(sites, dtype=jnp.int32)
    cosine, sine = phases(momenta, flat_index, sites * tiles // PLANE)
    cosine = (cosine * norm).reshape(moms, chunks, LANES).transpose(1, 0, 2)
    sine = (sine * norm).reshape(moms, chunks, LANES).transpose(1, 0, 2)

    width = moms * disps * nv
    one = lambda shape: pl.BlockSpec((1,) + shape, lambda i: (i,) + (0,) * len(shape))
    depth = 6 * LANES
    partial = pl.pallas_call(
        contract_kernel,
        grid=(chunks,),
        out_shape=jax.ShapeDtypeStruct((2 * row_count, width), jnp.float32),
        in_specs=[
            pl.BlockSpec(memory_space=pltpu.SMEM),
            one((6, row_count, LANES)),
            vmem,
            vmem,
            vmem,
            one((moms, LANES)),
            one((moms, LANES)),
        ],
        out_specs=pl.BlockSpec((2 * row_count, width), lambda i: (0, 0)),
        scratch_shapes=[
            pltpu.VMEM((disps, 6, nv, LANES), jnp.float32),
            pltpu.VMEM((2 * row_count, depth), jnp.bfloat16),
            pltpu.VMEM((2 * row_count, depth), jnp.bfloat16),
            pltpu.VMEM((width, depth), jnp.bfloat16),
            pltpu.VMEM((width, depth), jnp.bfloat16),
        ],
        compiler_params=pltpu.CompilerParams(vmem_limit_bytes=VMEM_LIMIT),
        name="contract",
    )(directions, rows, cols, own_links, own_back, cosine, sine)

    partial = partial.reshape(2, row_count, width)
    mine = lax.psum_scatter(partial, "tile", scatter_dimension=1, tiled=True)
    mine = mine.reshape(2, row_count // tiles, moms, disps, nv)
    return mine.transpose(1, 3, 0, 2, 4)


def solution(mesh):
    return jax.shard_map(
        local,
        mesh=mesh,
        in_specs=(
            P(None, "vec", None, ("groups", "tile")),
            P(None, None, None, None, ("groups", "tile")),
            P(),
            P(),
        ),
        out_specs=P(("groups", "tile"), None, None, None, "vec"),
        check_vma=False,
    )
```

time: 785 us -> 314 us (0.40)
  local copies, waits for them, and re-layouts: 274 us -> 17.7 us
  other arithmetic: 126 us -> 1.14 us
  matrix products: 122 us -> 0 us
  blocking collectives: 0 us -> 122 us
  waiting for transfers between devices: 201 us -> 83.8 us
  Pallas kernels: 0 us -> 68.2 us
  loops' own time: 18.9 us -> 0 us
  starting transfers between devices: 19.4 us -> 6.52 us
    ppermute x11 -> x0, waiting for transfers between devices: 158 us -> none  [the longest x5 70.6 us: extended(): before = lax.ppermute(last, axis, up)]
    slice x99 -> x4, local copies, waits for them, and re-layouts: 126 us -> 3.98 us  [the longest x2 2.49 us: local(): before = jnp.roll(slabs[:, chunks - PER_PLANE:], 1, axis=0)]
    dot_general x8 -> x0, matrix products: 122 us -> none  [one_momentum(): jnp.einsum('ik,dcjk->idcj', left_flat, right_mat, precision=lax.Precision...]
    all_to_all x0 -> x1, blocking collectives: none -> 70.4 us  [local(): slabs = lax.all_to_all(slabs, 'tile', 0, 0)]
    pallas_call x0 -> x2, Pallas kernels: none -> 68.2 us  [the longest x1 41.1 us: local(): pl.pallas_call(contract_kernel, grid=(chunks,), out_shape=jax.ShapeDtypeS...]
    squeeze x41 -> x0, local copies, waits for them, and re-layouts: 61.5 us -> none  [the longest x16 48.1 us: twist_left(): twisted_real = cos_row * left_field[0] - sin_row * left_field[1]]
    all_gather x0 -> x1, blocking collectives: none -> 51.7 us  [local(): all_links = lax.all_gather(own_links, 'tile', axis=0, tiled=True)]
    reduce_scatter x0 -> x1, waiting for transfers between devices: none -> 43.8 us  [local(): mine = lax.psum_scatter(partial, 'tile', scatter_dimension=1, tiled=True)]
  transfers between devices with their start and end apart: 13 -> 3, of which waited for: 10 -> 2; matrix products, arithmetic and copies ran while one was open for 9% -> 2% of each run, Pallas kernels for 0% -> 0%
where the time goes in v1:
time: 314 us; the launch traced here: 313 us
  blocking collectives  122 us (39%)
  waiting for transfers between devices  83.8 us (27%)
  Pallas kernels  68.2 us (22%)
  local copies, waits for them, and re-layouts  17.7 us (6%)
  between operations  13.5 us (4%)
  starting transfers between devices  6.52 us (2%)
    all_to_all x1, blocking collectives, local(): slabs = lax.all_to_all(slabs, 'tile', 0, 0)  70.4 us
    all_gather x1, blocking collectives, local(): all_links = lax.all_gather(own_links, 'tile', axis=0, tiled=True)  51.7 us
    reduce_scatter x1, waiting for transfers between devices, local(): mine = lax.psum_scatter(partial, 'tile', scatter_dimension=1, tiled=True)  43.8 us
    pallas_call x1, Pallas kernels, local(): pl.pallas_call(contract_kernel, grid=(chunks,), out_shape=jax.ShapeDtypeS...  41.1 us
    all_gather x1, waiting for transfers between devices, local(): lax.all_gather(cols[PER_PLANE:PER_PLANE + chunks], 'vec', axis=2, tiled=T...  40 us
    pallas_call x1, Pallas kernels, local(): pl.pallas_call(filter_kernel, out_shape=(jax.ShapeDtypeStruct(field.shape...  27.2 us
    all_to_all x1, starting transfers between devices, local(): field = lax.all_to_all(field, 'tile', 0, 0)  6.48 us
  transfers between devices with their start and end apart: 3, of which 2 were waited for; matrix products, arithmetic and copies ran while one was open for 2% of the time, Pallas kernels for 0%

profile of v1, /device:TPU:0, one launch (start us, length us, event | category | flops | bytes accessed | tf_op | source)
XLA Modules:
  0.0 313.0 jit_solution(11918011183538233194)
XLA Ops:
  6.5 1.7 copy.29
  8.3 1.4 copy.20
  9.7 6.5 %all-to-all-start = ((f32[4,8,6,16,128]{4,3,2,1,0:T(8,128)}), f32[4,8,6,16,128]{4,3,2,1,0:T(8,128)S(1)}, u32[]{:S(2)}, u32[]{:S(2)}) async-start(f32[4,8,6,16,128]{4,3,2,1,0:T(8,128)} %bitcast.1), calls=%async_computation | async-start | bytes 3145728 | tf_op jit(solution)/shard_map/all_to_all | solution.py:223
  16.2 0.1 copy.21
  16.3 0.1 reshape.150
  16.5 51.7 %all_gather.6 = f32[32,3,18,128]{3,0,2,1:T(8,128)S(1)} all-gather(f32[8,3,18,128]{3,0,2,1:T(8,128)S(1)} %bitcast.38), channel_id=1, replica_groups=mesh['groups'=2,'tile'=4,'vec'=4] {'tile'}, dimensions={0}, use_global_device_ids=true | all-gather | bytes 1105920 | tf_op jit(solution)/shard_map/all_gather | solution.py:226
  68.2 1.5 copy.24.links_ref
  69.7 1.2 copy-done
  70.9 27.2 %filter.1 = (f32[32,6,16,128]{3,2,1,0:T(8,128)}, f32[32,3,18,128]{3,2,1,0:T(8,128)}) custom-call(f32[32,6,16,128]{3,2,1,0:T(8,128)} %bitcast.33, f32[32,3,18,128]{3,2,1,0:T(8,128)} %copy.24.links_ref), custom_call_target="tpu_custom_call" | custom-call | tf_op jit(solution)/shard_map/filter/pallas_call | solution.py:229
  98.1 1.2 fusion.17
  99.2 1.3 fusion.18
  100.6 0.2 maximum_maximum_fusion
  100.8 70.4 %all_to_all.10 = f32[4,16,6,16,128]{4,3,2,1,0:T(8,128)S(1)} all-to-all(f32[4,16,6,16,128]{4,3,2,1,0:T(8,128)S(1)} %maximum_maximum_fusion), channel_id=1, replica_groups=mesh['groups'=2,'tile'=4,'vec'=4] {'tile'}, dimensions={0} | all-to-all | bytes 6291456 | tf_op jit(solution)/shard_map/all_to_all | solution.py:246
  171.2 0.1 slice.50
  171.3 1.4 copy.25
  172.8 0.8 copy.31
  173.6 0.9 sine_multiply_fusion
  174.5 1.7 constant_dynamic-slice_fusion.back_ref
  176.2 2.2 copy.26
  178.3 40.0 %all-gather.2.cloned.1.call-done.rows_ref = f32[8,6,256,128]{3,2,1,0:T(8,128)} async-done(((f32[8,6,64,128]{3,2,1,0:T(8,128)}), f32[8,6,256,128]{3,2,1,0:T(8,128)}) %all-gather.2.cloned.1.call-update) | async-done | bytes 6291472 | tf_op jit(solution)/shard_map/all_gather | solution.py:249
  218.3 41.1 %contract.1 = f32[512,1024]{1,0:T(8,128)} custom-call(s32[2]{0:T(128)} %dirs_ref.1, f32[8,6,256,128]{3,2,1,0:T(8,128)} %all-gather.2.cloned.1.call-done.rows_ref, f32[16,6,64,128]{3,2,1,0:T(8,128)} %bitcast.29, f32[8,3,18,128]{3,2,1,0:T(8,128)} %bitcast.40, f32[8,3,18,128]{3,2,1,0:T(8,128)} %constant_dynamic-slice_fusion.back_ref, ...), custom_call_target="tpu_custom_call" | custom-call | tf_op jit(solution)/shard_map/contract/pallas_call | solution.py:263
  259.4 43.8 %reduce-scatter.2.cloned.1.call-done = f32[2,64,1024]{2,1,0:T(8,128)} async-done(((f32[2,256,1024]{2,1,0:T(8,128)}), f32[2,64,1024]{2,1,0:T(8,128)}) %reduce-scatter.2.cloned.1.call-update) | async-done | bytes 524304 | tf_op jit(solution)/shard_map/reduce_scatter | solution.py:289
  303.2 1.8 reshape.154
  305.0 1.1 copy.27
  (15 shorter events, 0.1 us)
Async XLA Ops:
  9.7 6.5 %copy-start.2 = (f32[3,2,3,3,1024]{4,1,3,2,0:T(2,128)S(1)}, f32[3,2,3,3,1024]{4,1,3,2,0:T(2,128)}, u32[]{:S(2)}) copy-start(f32[3,2,3,3,1024]{4,1,3,2,0:T(2,128)} %param.5) | copy-start | bytes 663556
  9.7 60.0 %all-to-all-start = ((f32[4,8,6,16,128]{4,3,2,1,0:T(8,128)}), f32[4,8,6,16,128]{4,3,2,1,0:T(8,128)S(1)}, u32[]{:S(2)}, u32[]{:S(2)}) async-start(f32[4,8,6,16,128]{4,3,2,1,0:T(8,128)} %bitcast.1), calls=%async_computation | async-start | bytes 3145728 | tf_op jit(solution)/shard_map/all_to_all | solution.py:223
  16.2 202.1 %all-gather.2.cloned.1.call-start = ((), (), s32[]{:S(2)}) async-start(), calls=%async_computation.3 | async-start | bytes 7864320 | tf_op jit(solution)/shard_map/all_gather | solution.py:249
  69.7 1.2 copy-start
  98.1 2.5 copy-start.1
  171.3 2.3 copy-start.3
  172.7 130.5 %reduce-scatter.2.cloned.1.call-start = ((), (), s32[]{:S(2)}) async-start(), calls=%async_computation.4 | async-start | bytes 2621440 | tf_op jit(solution)/shard_map/reduce_scatter | solution.py:289
Sparse Core Ops, SparseCore 0:
  172.8 45.4 all-gather.1
  259.5 43.6 reduce-scatter.1

commit v2 on v1

--- a/solution.py
+++ b/solution.py
@@ -81,16 +81,29 @@
     return [shift_z(read(chunk, comp), step) for comp in range(6)]
 
 
-def filter_kernel(field_ref, links_ref, out_ref, back_ref, first, second):
-    chunks = field_ref.shape[0]
+def filter_kernel(count, me_ref, *refs):
+    pieces, refs = refs[:count], refs[count:]
+    all_links = refs[0]
+    outs, refs = refs[1 : 1 + count], refs[1 + count :]
+    own_back, field, first, second, links, back = refs
+    chunks = field.shape[0]
+    slab = chunks // count
+    start = me_ref[0] * slab
+
+    for index in range(count):
+        field[index * slab : (index + 1) * slab] = pieces[index][...]
 
     @pl.loop(0, chunks)
     def _(chunk):
-        back_ref[chunk, 0] = links_ref[(chunk - PER_PLANE + chunks) % chunks, 0]
-        back_ref[chunk, 1] = shift_y(
-            links_ref[chunk, 1], links_ref[in_plane(chunk, -1), 1], -1
-        )
-        back_ref[chunk, 2] = shift_z(links_ref[chunk, 2], -1)
+        links[chunk] = all_links[(chunk + start) % chunks]
+
+    @pl.loop(0, chunks)
+    def _(chunk):
+        back[chunk, 0] = links[(chunk - PER_PLANE + chunks) % chunks, 0]
+        back[chunk, 1] = shift_y(links[chunk, 1], links[in_plane(chunk, -1), 1], -1)
+        back[chunk, 2] = shift_z(links[chunk, 2], -1)
+
+    own_back[...] = back[0:slab]
 
     def hop(source, previous, target):
         @pl.loop(0, chunks)
@@ -99,11 +112,11 @@
             total = [None] * 6
             for spatial in range(3):
                 ahead = moved(read, chunk, spatial, 1, (chunk + PER_PLANE) % chunks)
-                total = apply_link(links_ref, chunk, spatial, False, ahead, total)
+                total = apply_link(links, chunk, spatial, False, ahead, total)
                 behind = moved(
                     read, chunk, spatial, -1, (chunk - PER_PLANE + chunks) % chunks
                 )
-                total = apply_link(back_ref, chunk, spatial, True, behind, total)
+                total = apply_link(back, chunk, spatial, True, behind, total)
             for comp in range(6):
                 if previous is None:
                     target[chunk, comp] = HOP_SCALE * total[comp]
@@ -112,12 +125,13 @@
                         2.0 * HOP_SCALE * total[comp] - previous[chunk, comp]
                     )
 
-    hop(field_ref, None, first)
-    older, newer = field_ref, first
-    for order in range(ITERS - 1):
-        target = out_ref if order == ITERS - 2 else (second if order % 2 == 0 else first)
-        hop(newer, older, target)
-        older, newer = newer, target
+    buffers = [field, first, second]
+    hop(field, None, first)
+    for order in range(1, ITERS):
+        hop(buffers[1], buffers[0], buffers[2])
+        buffers = [buffers[1], buffers[2], buffers[0]]
+    for index in range(count):
+        outs[index][...] = buffers[1][index * slab : (index + 1) * slab]
 
 
 def split(value):
@@ -126,37 +140,48 @@
     return high, low
 
 
-def contract_kernel(
-    dirs_ref, rows_ref, cols_ref, links_ref, back_ref, cos_ref, sin_ref,
-    out_ref, shifted, left_hi, left_lo, right_hi, right_lo,
-):
+def contract_kernel(groups, me_ref, dirs_ref, *refs):
+    rows_refs, refs = refs[:groups], refs[groups:]
+    cols_refs, refs = refs[:groups], refs[groups:]
+    links_ref, back_ref, cos_ref, sin_ref, out_ref = refs[:5]
+    staged, shifted, left_hi, left_lo, right_hi, right_lo = refs[5:]
     chunk = pl.program_id(0)
     disps = shifted.shape[0]
-    columns = cols_ref.shape[2]
-    row_count = rows_ref.shape[2]
+    columns = shifted.shape[2]
+    row_count = staged.shape[1]
     momenta = cos_ref.shape[1]
-    read = lambda at, comp: cols_ref[at + PER_PLANE, comp]
-
-    for disp in range(disps):
-        for heading in range(6):
-            @pl.when(dirs_ref[disp] == heading)
-            def _(disp=disp, heading=heading):
-                spatial = heading % 3
-                step = 1 if heading < 3 else -1
-                for block in range(0, columns, 16):
-                    stop = min(columns, block + 16)
-                    part = lambda at, comp: cols_ref[at + PER_PLANE, comp, block:stop, :]
-                    source = moved(part, chunk, spatial, step, chunk + step * PER_PLANE)
-                    table = links_ref if step > 0 else back_ref
-                    total = apply_link(table, chunk, spatial, step < 0, source, [None] * 6)
-                    for comp in range(6):
-                        shifted[disp, comp, block:stop, :] = total[comp]
+    tiles = cols_refs[0].shape[0]
+    size = cols_refs[0].shape[3]
+    share = size * groups
+
+    @pl.loop(0, tiles)
+    def _(turn):
+        home = (me_ref[0] - turn + tiles) % tiles * share
+        for group in range(groups):
+            rows_ref, cols_ref = rows_refs[group], cols_refs[group]
+            at = pl.ds(pl.multiple_of(home + group * size, size), size)
+            for piece in range(rows_ref.shape[0]):
+                place = pl.multiple_of(home + piece * columns + group * size, size)
+                for comp in range(6):
+                    staged[comp, pl.ds(place, size), :] = rows_ref[piece, turn, 0, comp]
+            part = lambda where, comp: cols_ref[turn, where + PER_PLANE, comp]
+            for disp in range(disps):
+                for heading in range(6):
+                    @pl.when(dirs_ref[disp] == heading)
+                    def _(disp=disp, heading=heading):
+                        spatial = heading % 3
+                        step = 1 if heading < 3 else -1
+                        source = moved(part, chunk, spatial, step, chunk + step * PER_PLANE)
+                        table = links_ref if step > 0 else back_ref
+                        total = apply_link(table, chunk, spatial, step < 0, source, [None] * 6)
+                        for comp in range(6):
+                            shifted[disp, comp, at, :] = total[comp]
 
     for colour in range(3):
         real_at = pl.ds(2 * colour * LANES, LANES)
         imag_at = pl.ds((2 * colour + 1) * LANES, LANES)
-        hi, lo = split(rows_ref[0, colour])
-        hi_i, lo_i = split(rows_ref[0, 3 + colour])
+        hi, lo = split(staged[colour])
+        hi_i, lo_i = split(staged[3 + colour])
         for half, store_r, store_i in ((left_hi, hi, hi_i), (left_lo, lo, lo_i)):
             half[0:row_count, real_at] = store_r
             half[0:row_count, imag_at] = store_i
@@ -217,77 +242,105 @@
     share = nv // tiles
     norm = 1.0 / math.sqrt(3.0 * sites * tiles)
     me = lax.axis_index("tile")
-
-    field = vectors.reshape(2, tiles, share, 3, chunks, LANES)
-    field = field.transpose(1, 4, 0, 3, 2, 5).reshape(tiles, chunks, 6, share, LANES)
-    field = lax.all_to_all(field, "tile", 0, 0)
-    field = field.reshape(every, 6, share, LANES)
+    here = me.reshape(1).astype(jnp.int32)
+    size = 8 if share % 8 == 0 else share
+    groups = share // size
+
+    def passed(value, steps):
+        if steps % tiles == 0:
+            return value
+        return lax.ppermute(value, "tile", [(i, (i + steps) % tiles) for i in range(tiles)])
+
     own_links = links.reshape(3, 18, chunks, LANES).transpose(2, 0, 1, 3)
     all_links = lax.all_gather(own_links, "tile", axis=0, tiled=True)
+    field = vectors.reshape(2, tiles, groups, size, 3, chunks, LANES)
+    field = field.transpose(2, 1, 5, 0, 4, 3, 6)
+    field = field.reshape(groups, tiles, chunks, 6, size, LANES)
 
     vmem = pl.BlockSpec(memory_space=pltpu.VMEM)
-    filtered, back = pl.pallas_call(
-        filter_kernel,
-        out_shape=(
-            jax.ShapeDtypeStruct(field.shape, jnp.float32),
-            jax.ShapeDtypeStruct(all_links.shape, jnp.float32),
+    smem = pl.BlockSpec(memory_space=pltpu.SMEM)
+    piece = jax.ShapeDtypeStruct((chunks, 6, size, LANES), jnp.float32)
+    whole_field = pltpu.VMEM((every, 6, size, LANES), jnp.float32)
+    whole_links = pltpu.VMEM(all_links.shape, jnp.float32)
+    run_filter = pl.pallas_call(
+        functools.partial(filter_kernel, tiles),
+        out_shape=(piece,) * tiles + (jax.ShapeDtypeStruct(own_links.shape, jnp.float32),),
+        in_specs=[smem] + [vmem] * (tiles + 1),
+        out_specs=(vmem,) * (tiles + 1),
+        scratch_shapes=[whole_field] * 3 + [whole_links] * 2,
+        compiler_params=pltpu.CompilerParams(vmem_limit_bytes=VMEM_LIMIT),
+        cost_estimate=pl.CostEstimate(
+            flops=12 * 10**9, bytes_accessed=2 * 10**6, transcendentals=0
         ),
-        in_specs=[vmem, vmem],
-        out_specs=(vmem, vmem),
-        scratch_shapes=[pltpu.VMEM(field.shape, jnp.float32)] * 2,
-        compiler_params=pltpu.CompilerParams(vmem_limit_bytes=VMEM_LIMIT),
         name="filter",
-    )(field, all_links)
-
-    slabs = filtered.reshape(tiles, chunks, 6, share, LANES)
-    before = jnp.roll(slabs[:, chunks - PER_PLANE :], 1, axis=0)
-    after = jnp.roll(slabs[:, :PER_PLANE], -1, axis=0)
-    slabs = jnp.concatenate([before, slabs, after], axis=1)
-    slabs = lax.all_to_all(slabs, "tile", 0, 0)
-    wide = chunks + 2 * PER_PLANE
-    cols = slabs.transpose(1, 2, 0, 3, 4).reshape(wide, 6, nv, LANES)
-    rows = lax.all_gather(
-        cols[PER_PLANE : PER_PLANE + chunks], "vec", axis=2, tiled=True
-    )
-    row_count = rows.shape[2]
-    own_back = lax.dynamic_slice_in_dim(back, me * chunks, chunks, 0)
+    )
+    rolled = jnp.stack(
+        [lax.dynamic_index_in_dim(field, (me + turn) % tiles, 1, False) for turn in range(tiles)]
+    )
+    slabs, gathered, own_back = [], [], None
+    received = [
+        [passed(rolled[turn, group], turn) for turn in range(tiles)] for group in range(groups)
+    ]
+    for group in range(groups):
+        ordered = [received[group][(tiles - turn) % tiles] for turn in range(tiles)]
+        *done, own_back = run_filter(here, *ordered, all_links)
+        back = jnp.stack([passed(done[turn], turn) for turn in range(tiles)])
+        slabs.append(back)
+        gathered.append(lax.all_gather(back, "vec", axis=0))
+    wide = []
+    for slab in slabs:
+        before = passed(slab[:, chunks - PER_PLANE :], 1)
+        after = passed(slab[:, :PER_PLANE], -1)
+        wide.append((before, slab, after))
+    for group, (before, slab, after) in enumerate(wide):
+        before = jnp.roll(before, 1, axis=0)
+        after = jnp.roll(after, -1, axis=0)
+        wide[group] = jnp.concatenate([before, slab, after], axis=1)
 
     flat_index = me * sites + jnp.arange(sites, dtype=jnp.int32)
     cosine, sine = phases(momenta, flat_index, sites * tiles // PLANE)
     cosine = (cosine * norm).reshape(moms, chunks, LANES).transpose(1, 0, 2)
     sine = (sine * norm).reshape(moms, chunks, LANES).transpose(1, 0, 2)
 
-    width = moms * disps * nv
+    row_count = nv * lax.axis_size("vec")
+    halves = 2
+    some = moms // halves
+    width = some * disps * nv
+    depth = 6 * LANES
     one = lambda shape: pl.BlockSpec((1,) + shape, lambda i: (i,) + (0,) * len(shape))
-    depth = 6 * LANES
-    partial = pl.pallas_call(
-        contract_kernel,
-        grid=(chunks,),
-        out_shape=jax.ShapeDtypeStruct((2 * row_count, width), jnp.float32),
-        in_specs=[
-            pl.BlockSpec(memory_space=pltpu.SMEM),
-            one((6, row_count, LANES)),
-            vmem,
-            vmem,
-            vmem,
-            one((moms, LANES)),
-            one((moms, LANES)),
-        ],
-        out_specs=pl.BlockSpec((2 * row_count, width), lambda i: (0, 0)),
-        scratch_shapes=[
-            pltpu.VMEM((disps, 6, nv, LANES), jnp.float32),
-            pltpu.VMEM((2 * row_count, depth), jnp.bfloat16),
-            pltpu.VMEM((2 * row_count, depth), jnp.bfloat16),
-            pltpu.VMEM((width, depth), jnp.bfloat16),
-            pltpu.VMEM((width, depth), jnp.bfloat16),
-        ],
-        compiler_params=pltpu.CompilerParams(vmem_limit_bytes=VMEM_LIMIT),
-        name="contract",
-    )(directions, rows, cols, own_links, own_back, cosine, sine)
-
-    partial = partial.reshape(2, row_count, width)
-    mine = lax.psum_scatter(partial, "tile", scatter_dimension=1, tiled=True)
-    mine = mine.reshape(2, row_count // tiles, moms, disps, nv)
+    row_block = pl.BlockSpec(
+        (row_count // nv, tiles, 1, 6, size, LANES), lambda i: (0, 0, i, 0, 0, 0)
+    )
+    parts = []
+    for half in range(halves):
+        pick = slice(half * some, (half + 1) * some)
+        partial = pl.pallas_call(
+            functools.partial(contract_kernel, groups),
+            grid=(chunks,),
+            out_shape=jax.ShapeDtypeStruct((2 * row_count, width), jnp.float32),
+            in_specs=[smem, smem]
+            + [row_block] * groups
+            + [vmem] * groups
+            + [vmem, vmem, one((some, LANES)), one((some, LANES))],
+            out_specs=pl.BlockSpec((2 * row_count, width), lambda i: (0, 0)),
+            scratch_shapes=[
+                pltpu.VMEM((6, row_count, LANES), jnp.float32),
+                pltpu.VMEM((disps, 6, nv, LANES), jnp.float32),
+                pltpu.VMEM((2 * row_count, depth), jnp.bfloat16),
+                pltpu.VMEM((2 * row_count, depth), jnp.bfloat16),
+                pltpu.VMEM((width, depth), jnp.bfloat16),
+                pltpu.VMEM((width, depth), jnp.bfloat16),
+            ],
+            compiler_params=pltpu.CompilerParams(vmem_limit_bytes=VMEM_LIMIT),
+            cost_estimate=pl.CostEstimate(
+                flops=20 * 10**9, bytes_accessed=12 * 10**6, transcendentals=0
+            ),
+            name="contract",
+        )(here, directions, *gathered, *wide, own_links, own_back, cosine[:, pick], sine[:, pick])
+        partial = partial.reshape(2, row_count, width)
+        mine = lax.psum_scatter(partial, "tile", scatter_dimension=1, tiled=True)
+        parts.append(mine.reshape(2, row_count // tiles, some, disps, nv))
+    mine = jnp.concatenate(parts, axis=2)
     return mine.transpose(1, 3, 0, 2, 4)
 
 

time: 314 us -> 300 us (0.955)
  blocking collectives: 122 us -> 33.3 us
  Pallas kernels: 68.2 us -> 110 us
  starting transfers between devices: 6.52 us -> 28.3 us
  waiting for transfers between devices: 83.8 us -> 95.2 us
  other arithmetic: 1.14 us -> 7.3 us
  local copies, waits for them, and re-layouts: 17.7 us -> 11.9 us
    all_to_all x1 -> x0, blocking collectives: 70.4 us -> none  [local(): slabs = lax.all_to_all(slabs, 'tile', 0, 0)]
    ppermute x0 -> x16, waiting for transfers between devices: none -> 67.4 us  [passed(): lax.ppermute(value, 'tile', [(i, (i + steps) % tiles) for i in range(tile...]
    pallas_call x2 -> x4, Pallas kernels: 68.2 us -> 110 us  [the longest x2 68.6 us: local(): pl.pallas_call(functools.partial(contract_kernel, groups), grid=(chunks,)...]
    all_gather x1 -> x2, waiting for transfers between devices: 40 us -> 0.01 us  [local(): gathered.append(lax.all_gather(back, 'vec', axis=0))]
    ppermute x0 -> x16, starting transfers between devices: none -> 28.1 us  [passed(): lax.ppermute(value, 'tile', [(i, (i + steps) % tiles) for i in range(tile...]
    all_gather x1, blocking collectives: 51.7 us -> 33.3 us  [local(): all_links = lax.all_gather(own_links, 'tile', axis=0, tiled=True)]
    reduce_scatter x1 -> x2, waiting for transfers between devices: 43.8 us -> 27.7 us  [local(): mine = lax.psum_scatter(partial, 'tile', scatter_dimension=1, tiled=True)]
    all_to_all x1 -> x0, starting transfers between devices: 6.48 us -> none  [local(): field = lax.all_to_all(field, 'tile', 0, 0)]
  transfers between devices with their start and end apart: 3 -> 20, of which waited for: 2 -> 11; matrix products, arithmetic and copies ran while one was open for 2% -> 4% of each run, Pallas kernels for 0% -> 18%
where the time goes in v2:
time: 300 us
  Pallas kernels  110 us (37%)
  waiting for transfers between devices  95.2 us (32%)
  blocking collectives  33.3 us (11%)
  starting transfers between devices  28.3 us (9%)
  between operations  13.4 us (4%)
  local copies, waits for them, and re-layouts  11.9 us (4%)
  other arithmetic  7.3 us (2%)
    pallas_call x2, Pallas kernels, local(): pl.pallas_call(functools.partial(contract_kernel, groups), grid=(chunks,)...  68.6 us
    ppermute x16, waiting for transfers between devices, passed(): lax.ppermute(value, 'tile', [(i, (i + steps) % tiles) for i in range(tile...  67.4 us
    pallas_call x2, Pallas kernels, local(): *done, own_back = run_filter(here, *ordered, all_links)  41.8 us
    all_gather x1, blocking collectives, local(): all_links = lax.all_gather(own_links, 'tile', axis=0, tiled=True)  33.3 us
    ppermute x16, starting transfers between devices, passed(): lax.ppermute(value, 'tile', [(i, (i + steps) % tiles) for i in range(tile...  28.1 us
    reduce_scatter x2, waiting for transfers between devices, local(): mine = lax.psum_scatter(partial, 'tile', scatter_dimension=1, tiled=True)  27.7 us
  transfers between devices with their start and end apart: 20, of which 11 were waited for; matrix products, arithmetic and copies ran while one was open for 4% of the time, Pallas kernels for 18%

profile of v2, /device:TPU:0, one launch (start us, length us, event | category | flops | bytes accessed | tf_op | source)
XLA Modules:
  0.0 299.8 jit_solution(8440960598810788350)
XLA Ops:
  8.3 5.1 %collective-permute-start.6 = (f32[8,6,8,128]{3,2,1,0:T(8,128)S(1)}, f32[8,6,8,128]{3,2,1,0:T(8,128)S(1)}, u32[]{:S(2)}, u32[]{:S(2)}) collective-permute-start(f32[8,6,8,128]{3,2,1,0:T(8,128)S(1)} %get-tuple-element.35), channel_id=1, source_target_pairs={{0,12},{4,0},{8,4},{12,8},{1,13},{5,1},{9,5},{13,9},{2,14},{6,2},{... | collective-permute-start | bytes 589832 | tf_op jit(solution)/shard_map/ppermute | solution.py:252
  14.9 33.3 %all_gather.15 = f32[32,3,18,128]{3,0,2,1:T(8,128)S(1)} all-gather(f32[8,3,18,128]{3,0,2,1:T(8,128)S(1)} %bitcast.54), channel_id=1, replica_groups=mesh['groups'=2,'tile'=4,'vec'=4] {'tile'}, dimensions={0}, use_global_device_ids=true | all-gather | bytes 1105920 | tf_op jit(solution)/shard_map/all_gather | solution.py:255
  51.3 20.9 %filter.3 = (f32[8,6,8,128]{3,2,1,0:T(8,128)}, f32[8,6,8,128]{3,2,1,0:T(8,128)}, f32[8,6,8,128]{3,2,1,0:T(8,128)}, f32[8,6,8,128]{3,2,1,0:T(8,128)}, f32[8,3,18,128]{3,2,1,0:T(8,128)}) custom-call(s32[1]{0:T(128)} %bitcast.me_ref, f32[8,6,8,128]{3,2,1,0:T(8,128)} %get-tuple-element.37.refs_0_, f32[8,6,8,128]{3,2,1,0:T(8,128)} %copy-done.6, ...), custom_call_target="tpu_custom_call" | custom-call | flops 12000000000 | bytes 2000000 | tf_op jit(solution)/shard_map/filter/pallas_call | solution.py:286
  73.5 2.5 collective-permute-start.11
  76.1 5.2 %collective-permute-done.9 = f32[8,6,8,128]{3,2,1,0:T(8,128)S(1)} collective-permute-done((f32[8,6,8,128]{3,2,1,0:T(8,128)}, f32[8,6,8,128]{3,2,1,0:T(8,128)S(1)}, u32[]{:S(2)}, u32[]{:S(2)}) %collective-permute-start.9) | collective-permute-done | bytes 196640 | tf_op jit(solution)/shard_map/ppermute | solution.py:252
  81.3 4.2 %collective-permute-done.10 = f32[8,6,8,128]{3,2,1,0:T(8,128)S(1)} collective-permute-done((f32[8,6,8,128]{3,2,1,0:T(8,128)}, f32[8,6,8,128]{3,2,1,0:T(8,128)S(1)}, u32[]{:S(2)}, u32[]{:S(2)}) %collective-permute-start.10) | collective-permute-done | bytes 196640 | tf_op jit(solution)/shard_map/ppermute | solution.py:252
  85.5 1.9 pad_maximum_fusion.1
  87.5 5.8 %collective-permute-start = (f32[8,6,8,128]{3,2,1,0:T(8,128)S(1)}, f32[8,6,8,128]{3,2,1,0:T(8,128)S(1)}, u32[]{:S(2)}, u32[]{:S(2)}) collective-permute-start(f32[8,6,8,128]{3,2,1,0:T(8,128)S(1)} %get-tuple-element.36), channel_id=1, source_target_pairs={{0,12},{4,0},{8,4},{12,8},{1,13},{5,1},{9,5},{13,9},{2,14},{6,2},{... | collective-permute-start | bytes 589832 | tf_op jit(solution)/shard_map/ppermute | solution.py:252
  93.9 4.6 %collective-permute-done.refs_1_ = f32[8,6,8,128]{3,2,1,0:T(8,128)S(1)} collective-permute-done((f32[8,6,8,128]{3,2,1,0:T(8,128)S(1)}, f32[8,6,8,128]{3,2,1,0:T(8,128)S(1)}, u32[]{:S(2)}, u32[]{:S(2)}) %collective-permute-start) | collective-permute-done | bytes 196640 | tf_op jit(solution)/shard_map/ppermute | solution.py:252
  98.6 12.6 %collective-permute-done.1.refs_2_ = f32[8,6,8,128]{3,2,1,0:T(8,128)S(1)} collective-permute-done((f32[8,6,8,128]{3,2,1,0:T(8,128)S(1)}, f32[8,6,8,128]{3,2,1,0:T(8,128)S(1)}, u32[]{:S(2)}, u32[]{:S(2)}) %collective-permute-start.1) | collective-permute-done | bytes 196640 | tf_op jit(solution)/shard_map/ppermute | solution.py:252
  111.9 20.9 %filter.2 = (f32[8,6,8,128]{3,2,1,0:T(8,128)}, f32[8,6,8,128]{3,2,1,0:T(8,128)}, f32[8,6,8,128]{3,2,1,0:T(8,128)}, f32[8,6,8,128]{3,2,1,0:T(8,128)}, f32[8,3,18,128]{3,2,1,0:T(8,128)}) custom-call(s32[1]{0:T(128)} %bitcast.me_ref, f32[8,6,8,128]{3,2,1,0:T(8,128)} %get-tuple-element.38.refs_0_, f32[8,6,8,128]{3,2,1,0:T(8,128)} %copy-done.9, ...), custom_call_target="tpu_custom_call" | custom-call | flops 12000000000 | bytes 2000000 | tf_op jit(solution)/shard_map/filter/pallas_call | solution.py:286
  132.9 3.7 %collective-permute-start.5 = (f32[8,6,8,128]{3,2,1,0:T(8,128)}, f32[8,6,8,128]{3,2,1,0:T(8,128)S(1)}, u32[]{:S(2)}, u32[]{:S(2)}) collective-permute-start(f32[8,6,8,128]{3,2,1,0:T(8,128)} %get-tuple-element.17), channel_id=1, source_target_pairs={{0,12},{4,0},{8,4},{12,8},{1,13},{5,1},{9,5},{13,9},{2,14},{6,2},{... | collective-permute-start | bytes 589832 | tf_op jit(solution)/shard_map/ppermute | solution.py:252
  136.7 6.1 %collective-permute-done.3 = f32[8,6,8,128]{3,2,1,0:T(8,128)S(1)} collective-permute-done((f32[8,6,8,128]{3,2,1,0:T(8,128)}, f32[8,6,8,128]{3,2,1,0:T(8,128)S(1)}, u32[]{:S(2)}, u32[]{:S(2)}) %collective-permute-start.3) | collective-permute-done | bytes 196640 | tf_op jit(solution)/shard_map/ppermute | solution.py:252
  142.7 6.7 %collective-permute-done.4 = f32[8,6,8,128]{3,2,1,0:T(8,128)S(1)} collective-permute-done((f32[8,6,8,128]{3,2,1,0:T(8,128)}, f32[8,6,8,128]{3,2,1,0:T(8,128)S(1)}, u32[]{:S(2)}, u32[]{:S(2)}) %collective-permute-start.4) | collective-permute-done | bytes 196640 | tf_op jit(solution)/shard_map/ppermute | solution.py:252
  149.4 1.9 pad_maximum_fusion
  152.5 3.9 %collective-permute-start.14 = (f32[4,4,6,8,128]{4,3,2,1,0:T(8,128)S(1)}, f32[4,4,6,8,128]{4,3,2,1,0:T(8,128)S(1)}, u32[]{:S(2)}, u32[]{:S(2)}) collective-permute-start(f32[4,4,6,8,128]{4,3,2,1,0:T(8,128)S(1)} %get-tuple-element.27), channel_id=1, source_target_pairs={{0,4},{4,8},{8,12},{12,0},{1,5},{5,9},{9,13},{13,1},{2,6},{6,10},{... | collective-permute-start | bytes 1179656 | tf_op jit(solution)/shard_map/ppermute | solution.py:252
  156.5 2.1 collective-permute-start.12
  161.6 4.8 %collective-permute-done.14 = f32[4,4,6,8,128]{4,3,2,1,0:T(8,128)S(1)} collective-permute-done((f32[4,4,6,8,128]{4,3,2,1,0:T(8,128)S(1)}, f32[4,4,6,8,128]{4,3,2,1,0:T(8,128)S(1)}, u32[]{:S(2)}, u32[]{:S(2)}) %collective-permute-start.14) | collective-permute-done | bytes 393248 | tf_op jit(solution)/shard_map/ppermute | solution.py:252
  166.4 8.5 %collective-permute-done.15 = f32[4,4,6,8,128]{4,3,2,1,0:T(8,128)S(1)} collective-permute-done((f32[4,4,6,8,128]{4,3,2,1,0:T(8,128)S(1)}, f32[4,4,6,8,128]{4,3,2,1,0:T(8,128)S(1)}, u32[]{:S(2)}, u32[]{:S(2)}) %collective-permute-start.15) | collective-permute-done | bytes 393248 | tf_op jit(solution)/shard_map/ppermute | solution.py:252
  174.9 8.3 %collective-permute-done.12 = f32[4,4,6,8,128]{4,3,2,1,0:T(8,128)S(1)} collective-permute-done((f32[4,4,6,8,128]{4,3,2,1,0:T(8,128)S(1)}, f32[4,4,6,8,128]{4,3,2,1,0:T(8,128)S(1)}, u32[]{:S(2)}, u32[]{:S(2)}) %collective-permute-start.12) | collective-permute-done | bytes 393248 | tf_op jit(solution)/shard_map/ppermute | solution.py:252
  183.3 6.4 %collective-permute-done.13 = f32[4,4,6,8,128]{4,3,2,1,0:T(8,128)S(1)} collective-permute-done((f32[4,4,6,8,128]{4,3,2,1,0:T(8,128)S(1)}, f32[4,4,6,8,128]{4,3,2,1,0:T(8,128)S(1)}, u32[]{:S(2)}, u32[]{:S(2)}) %collective-permute-start.13) | collective-permute-done | bytes 393248 | tf_op jit(solution)/shard_map/ppermute | solution.py:252
  192.5 34.3 %contract.2 = f32[512,512]{1,0:T(8,128)} custom-call(s32[1]{0:T(128)} %bitcast.me_ref, s32[2]{0:T(128)} %dirs_ref.3, f32[4,4,8,6,8,128]{5,4,3,2,1,0:T(8,128)} %bitcast.78, f32[4,4,8,6,8,128]{5,4,3,2,1,0:T(8,128)} %bitcast.76, f32[4,16,6,8,128]{4,3,2,1,0:T(8,128)} %maximum_maximum_fusion.refs_2_, f32[4,16,6,8,128]{4,3,2,1,0:T(8,128)} %maximum_maximum_fusion.1.refs_3_, ...), custom_call_target="tpu_custom_call" | custom-call | flops 20000000000 | bytes 12000000 | tf_op jit(solution)/shard_map/contract/pallas_call | solution.py:317
  226.9 34.3 %contract.3 = f32[512,512]{1,0:T(8,128)} custom-call(s32[1]{0:T(128)} %bitcast.me_ref, s32[2]{0:T(128)} %dirs_ref.3, f32[4,4,8,6,8,128]{5,4,3,2,1,0:T(8,128)} %bitcast.79, f32[4,4,8,6,8,128]{5,4,3,2,1,0:T(8,128)} %bitcast.77, f32[4,16,6,8,128]{4,3,2,1,0:T(8,128)} %maximum_maximum_fusion.refs_2_, f32[4,16,6,8,128]{4,3,2,1,0:T(8,128)} %maximum_maximum_fusion.1.refs_3_, ...), custom_call_target="tpu_custom_call" | custom-call | flops 20000000000 | bytes 12000000 | tf_op jit(solution)/shard_map/contract/pallas_call | solution.py:317
  262.6 27.7 %reduce-scatter.5.cloned.1.call-done = f32[2,64,512]{2,1,0:T(8,128)} async-done(((f32[2,256,512]{2,1,0:T(8,128)}), f32[2,64,512]{2,1,0:T(8,128)}) %reduce-scatter.5.cloned.1.call-update) | async-done | bytes 262160 | tf_op jit(solution)/shard_map/reduce_scatter | solution.py:341
  (83 shorter events, 20.7 us)
Async XLA Ops:
  6.5 186.0 %all-gather.7.cloned.1.call-start = ((), (), s32[]{:S(2)}) async-start(), calls=%async_computation.5 | async-start | bytes 3932160 | tf_op jit(solution)/shard_map/all_gather | solution.py:289
  8.3 42.2 %collective-permute-start.6 = (f32[8,6,8,128]{3,2,1,0:T(8,128)S(1)}, f32[8,6,8,128]{3,2,1,0:T(8,128)S(1)}, u32[]{:S(2)}, u32[]{:S(2)}) collective-permute-start(f32[8,6,8,128]{3,2,1,0:T(8,128)S(1)} %get-tuple-element.35), channel_id=1, source_target_pairs={{0,12},{4,0},{8,4},{12,8},{1,13},{5,1},{9,5},{13,9},{2,14},{6,2},{... | collective-permute-start | bytes 589832 | tf_op jit(solution)/shard_map/ppermute | solution.py:252
  13.4 37.1 %collective-permute-start.7 = (f32[8,6,8,128]{3,2,1,0:T(8,128)S(1)}, f32[8,6,8,128]{3,2,1,0:T(8,128)S(1)}, u32[]{:S(2)}, u32[]{:S(2)}) collective-permute-start(f32[8,6,8,128]{3,2,1,0:T(8,128)S(1)} %get-tuple-element.33), channel_id=1, source_target_pairs={{0,8},{4,12},{8,0},{12,4},{1,9},{5,13},{9,1},{13,5},{2,10},{6,14},... | collective-permute-start | bytes 589832 | tf_op jit(solution)/shard_map/ppermute | solution.py:252
  13.6 37.0 %collective-permute-start.8 = (f32[8,6,8,128]{3,2,1,0:T(8,128)S(1)}, f32[8,6,8,128]{3,2,1,0:T(8,128)S(1)}, u32[]{:S(2)}, u32[]{:S(2)}) collective-permute-start(f32[8,6,8,128]{3,2,1,0:T(8,128)S(1)} %get-tuple-element.31), channel_id=1, source_target_pairs={{0,4},{4,8},{8,12},{12,0},{1,5},{5,9},{9,13},{13,1},{2,6},{6,10},{... | collective-permute-start | bytes 589832 | tf_op jit(solution)/shard_map/ppermute | solution.py:252
  72.2 9.0 %collective-permute-start.9 = (f32[8,6,8,128]{3,2,1,0:T(8,128)}, f32[8,6,8,128]{3,2,1,0:T(8,128)S(1)}, u32[]{:S(2)}, u32[]{:S(2)}) collective-permute-start(f32[8,6,8,128]{3,2,1,0:T(8,128)} %get-tuple-element.19), channel_id=1, source_target_pairs={{0,4},{4,8},{8,12},{12,0},{1,5},{5,9},{9,13},{13,1},{2,6},{6,10},{... | collective-permute-start | bytes 589832 | tf_op jit(solution)/shard_map/ppermute | solution.py:252
  72.2 13.3 %collective-permute-start.10 = (f32[8,6,8,128]{3,2,1,0:T(8,128)}, f32[8,6,8,128]{3,2,1,0:T(8,128)S(1)}, u32[]{:S(2)}, u32[]{:S(2)}) collective-permute-start(f32[8,6,8,128]{3,2,1,0:T(8,128)} %get-tuple-element.20), channel_id=1, source_target_pairs={{0,8},{4,12},{8,0},{12,4},{1,9},{5,13},{9,1},{13,5},{2,10},{6,14},... | collective-permute-start | bytes 589832 | tf_op jit(solution)/shard_map/ppermute | solution.py:252
  73.5 12.0 %collective-permute-start.11 = (f32[8,6,8,128]{3,2,1,0:T(8,128)}, f32[8,6,8,128]{3,2,1,0:T(8,128)S(1)}, u32[]{:S(2)}, u32[]{:S(2)}) collective-permute-start(f32[8,6,8,128]{3,2,1,0:T(8,128)} %get-tuple-element.21), channel_id=1, source_target_pairs={{0,12},{4,0},{8,4},{12,8},{1,13},{5,1},{9,5},{13,9},{2,14},{6,2},{... | collective-permute-start | bytes 589832 | tf_op jit(solution)/shard_map/ppermute | solution.py:252
  87.4 105.1 %all-gather.5.cloned.1.call-start = ((), (), s32[]{:S(2)}) async-start(), calls=%async_computation.4 | async-start | bytes 3932160 | tf_op jit(solution)/shard_map/all_gather | solution.py:289
  87.5 11.1 %collective-permute-start = (f32[8,6,8,128]{3,2,1,0:T(8,128)S(1)}, f32[8,6,8,128]{3,2,1,0:T(8,128)S(1)}, u32[]{:S(2)}, u32[]{:S(2)}) collective-permute-start(f32[8,6,8,128]{3,2,1,0:T(8,128)S(1)} %get-tuple-element.36), channel_id=1, source_target_pairs={{0,12},{4,0},{8,4},{12,8},{1,13},{5,1},{9,5},{13,9},{2,14},{6,2},{... | collective-permute-start | bytes 589832 | tf_op jit(solution)/shard_map/ppermute | solution.py:252
  93.3 17.9 %collective-permute-start.1 = (f32[8,6,8,128]{3,2,1,0:T(8,128)S(1)}, f32[8,6,8,128]{3,2,1,0:T(8,128)S(1)}, u32[]{:S(2)}, u32[]{:S(2)}) collective-permute-start(f32[8,6,8,128]{3,2,1,0:T(8,128)S(1)} %get-tuple-element.34), channel_id=1, source_target_pairs={{0,8},{4,12},{8,0},{12,4},{1,9},{5,13},{9,1},{13,5},{2,10},{6,14},... | collective-permute-start | bytes 589832 | tf_op jit(solution)/shard_map/ppermute | solution.py:252
  93.7 17.4 %collective-permute-start.2 = (f32[8,6,8,128]{3,2,1,0:T(8,128)S(1)}, f32[8,6,8,128]{3,2,1,0:T(8,128)S(1)}, u32[]{:S(2)}, u32[]{:S(2)}) collective-permute-start(f32[8,6,8,128]{3,2,1,0:T(8,128)S(1)} %get-tuple-element.32), channel_id=1, source_target_pairs={{0,4},{4,8},{8,12},{12,0},{1,5},{5,9},{9,13},{13,1},{2,6},{6,10},{... | collective-permute-start | bytes 589832 | tf_op jit(solution)/shard_map/ppermute | solution.py:252
  98.6 12.6 %copy-start.9 = (f32[8,6,8,128]{3,2,1,0:T(8,128)}, f32[8,6,8,128]{3,2,1,0:T(8,128)S(1)}, u32[]{:S(2)}) copy-start(f32[8,6,8,128]{3,2,1,0:T(8,128)S(1)} %collective-permute-done.refs_1_) | copy-start | bytes 589828
  132.8 19.4 %copy-start.5 = (s32[8,3]{0,1:T(4,128)S(1)}, s32[8,3]{0,1:T(4,128)}, u32[]{:S(2)}) copy-start(s32[8,3]{0,1:T(4,128)} %param.6) | copy-start | bytes 292
  132.8 19.6 %copy-start = (f32[4,8,6,8,128]{4,3,2,1,0:T(8,128)S(1)}, f32[4,8,6,8,128]{4,3,2,1,0:T(8,128)}, u32[]{:S(2)}) copy-start(f32[4,8,6,8,128]{4,3,2,1,0:T(8,128)} %pad_maximum_fusion.1) | copy-start | bytes 2359300
  132.8 9.9 %collective-permute-start.3 = (f32[8,6,8,128]{3,2,1,0:T(8,128)}, f32[8,6,8,128]{3,2,1,0:T(8,128)S(1)}, u32[]{:S(2)}, u32[]{:S(2)}) collective-permute-start(f32[8,6,8,128]{3,2,1,0:T(8,128)} %get-tuple-element.15), channel_id=1, source_target_pairs={{0,4},{4,8},{8,12},{12,0},{1,5},{5,9},{9,13},{13,1},{2,6},{6,10},{... | collective-permute-start | bytes 589832 | tf_op jit(solution)/shard_map/ppermute | solution.py:252
  132.9 16.5 %collective-permute-start.4 = (f32[8,6,8,128]{3,2,1,0:T(8,128)}, f32[8,6,8,128]{3,2,1,0:T(8,128)S(1)}, u32[]{:S(2)}, u32[]{:S(2)}) collective-permute-start(f32[8,6,8,128]{3,2,1,0:T(8,128)} %get-tuple-element.16), channel_id=1, source_target_pairs={{0,8},{4,12},{8,0},{12,4},{1,9},{5,13},{9,1},{13,5},{2,10},{6,14},... | collective-permute-start | bytes 589832 | tf_op jit(solution)/shard_map/ppermute | solution.py:252
  132.9 16.5 %collective-permute-start.5 = (f32[8,6,8,128]{3,2,1,0:T(8,128)}, f32[8,6,8,128]{3,2,1,0:T(8,128)S(1)}, u32[]{:S(2)}, u32[]{:S(2)}) collective-permute-start(f32[8,6,8,128]{3,2,1,0:T(8,128)} %get-tuple-element.17), channel_id=1, source_target_pairs={{0,12},{4,0},{8,4},{12,8},{1,13},{5,1},{9,5},{13,9},{2,14},{6,2},{... | collective-permute-start | bytes 589832 | tf_op jit(solution)/shard_map/ppermute | solution.py:252
  151.3 110.0 %reduce-scatter.3.cloned.1.call-start = ((), (), s32[]{:S(2)}) async-start(), calls=%async_computation.2 | async-start | bytes 1310720 | tf_op jit(solution)/shard_map/reduce_scatter | solution.py:341
  152.5 13.9 %collective-permute-start.14 = (f32[4,4,6,8,128]{4,3,2,1,0:T(8,128)S(1)}, f32[4,4,6,8,128]{4,3,2,1,0:T(8,128)S(1)}, u32[]{:S(2)}, u32[]{:S(2)}) collective-permute-start(f32[4,4,6,8,128]{4,3,2,1,0:T(8,128)S(1)} %get-tuple-element.27), channel_id=1, source_target_pairs={{0,4},{4,8},{8,12},{12,0},{1,5},{5,9},{9,13},{13,1},{2,6},{6,10},{... | collective-permute-start | bytes 1179656 | tf_op jit(solution)/shard_map/ppermute | solution.py:252
  156.4 18.5 %collective-permute-start.15 = (f32[4,4,6,8,128]{4,3,2,1,0:T(8,128)S(1)}, f32[4,4,6,8,128]{4,3,2,1,0:T(8,128)S(1)}, u32[]{:S(2)}, u32[]{:S(2)}) collective-permute-start(f32[4,4,6,8,128]{4,3,2,1,0:T(8,128)S(1)} %get-tuple-element.28), channel_id=1, source_target_pairs={{0,12},{4,0},{8,4},{12,8},{1,13},{5,1},{9,5},{13,9},{2,14},{6,2},{... | collective-permute-start | bytes 1179656 | tf_op jit(solution)/shard_map/ppermute | solution.py:252
  156.5 26.8 %collective-permute-start.12 = (f32[4,4,6,8,128]{4,3,2,1,0:T(8,128)S(1)}, f32[4,4,6,8,128]{4,3,2,1,0:T(8,128)S(1)}, u32[]{:S(2)}, u32[]{:S(2)}) collective-permute-start(f32[4,4,6,8,128]{4,3,2,1,0:T(8,128)S(1)} %get-tuple-element.29), channel_id=1, source_target_pairs={{0,4},{4,8},{8,12},{12,0},{1,5},{5,9},{9,13},{13,1},{2,6},{6,10},{... | collective-permute-start | bytes 1179656 | tf_op jit(solution)/shard_map/ppermute | solution.py:252
  158.5 31.2 %collective-permute-start.13 = (f32[4,4,6,8,128]{4,3,2,1,0:T(8,128)S(1)}, f32[4,4,6,8,128]{4,3,2,1,0:T(8,128)S(1)}, u32[]{:S(2)}, u32[]{:S(2)}) collective-permute-start(f32[4,4,6,8,128]{4,3,2,1,0:T(8,128)S(1)} %get-tuple-element.30), channel_id=1, source_target_pairs={{0,12},{4,0},{8,4},{12,8},{1,13},{5,1},{9,5},{13,9},{2,14},{6,2},{... | collective-permute-start | bytes 1179656 | tf_op jit(solution)/shard_map/ppermute | solution.py:252
  161.6 28.2 %copy-start.2 = (f32[8,6,8,128]{3,2,1,0:T(8,128)S(1)}, f32[8,6,8,128]{3,2,1,0:T(8,128)}, u32[]{:S(2)}) copy-start(f32[8,6,8,128]{3,2,1,0:T(8,128)} %get-tuple-element.18) | copy-start | bytes 589828
  226.8 63.4 %reduce-scatter.5.cloned.1.call-start = ((), (), s32[]{:S(2)}) async-start(), calls=%async_computation.3 | async-start | bytes 1310720 | tf_op jit(solution)/shard_map/reduce_scatter | solution.py:341
  (8 other events, 16.5 us)
Sparse Core Ops, SparseCore 0:
  87.6 31.8 all-gather.6
  151.4 29.9 all-gather.4
  227.0 28.8 reduce-scatter.2
  261.4 28.8 reduce-scatter.4

commit v3 on v2

--- a/solution.py
+++ b/solution.py
@@ -140,42 +140,51 @@
     return high, low
 
 
-def contract_kernel(groups, me_ref, dirs_ref, *refs):
-    rows_refs, refs = refs[:groups], refs[groups:]
-    cols_refs, refs = refs[:groups], refs[groups:]
-    links_ref, back_ref, cos_ref, sin_ref, out_ref = refs[:5]
-    staged, shifted, left_hi, left_lo, right_hi, right_lo = refs[5:]
+def displace_kernel(me_ref, dirs_ref, cols_ref, links_ref, back_ref, out_ref):
+    chunks, disps = out_ref.shape[0], out_ref.shape[1]
+    tiles, size = cols_ref.shape[0], cols_ref.shape[3]
+    unrolled = min(tiles, 4)
+    for disp in range(disps):
+        for heading in range(6):
+            @pl.when(dirs_ref[disp] == heading)
+            def _(disp=disp, heading=heading):
+                spatial = heading % 3
+                step = 1 if heading < 3 else -1
+                table = links_ref if step > 0 else back_ref
+
+                @pl.loop(0, chunks * (tiles // unrolled))
+                def _(index):
+                    chunk = index % chunks
+                    results = []
+                    for inner in range(unrolled):
+                        turn = index // chunks * unrolled + inner
+                        part = lambda where, comp: cols_ref[turn, where + PER_PLANE, comp]
+                        source = moved(part, chunk, spatial, step, chunk + step * PER_PLANE)
+                        total = apply_link(table, chunk, spatial, step < 0, source, [None] * 6)
+                        results.append((turn, total))
+                    for turn, total in results:
+                        home = pl.multiple_of((me_ref[0] - turn + tiles) % tiles * size, size)
+                        for comp in range(6):
+                            out_ref[chunk, disp, comp, pl.ds(home, size), :] = total[comp]
+
+
+def contract_kernel(me_ref, rows_ref, shifted_ref, cos_ref, sin_ref, out_ref, *scratch):
+    staged, left_hi, left_lo, right_hi, right_lo = scratch
+    shifted = shifted_ref.at[0]
     chunk = pl.program_id(0)
-    disps = shifted.shape[0]
-    columns = shifted.shape[2]
+    disps = shifted_ref.shape[1]
+    columns = shifted_ref.shape[3]
     row_count = staged.shape[1]
     momenta = cos_ref.shape[1]
-    tiles = cols_refs[0].shape[0]
-    size = cols_refs[0].shape[3]
-    share = size * groups
+    tiles, size = rows_ref.shape[1], rows_ref.shape[4]
 
     @pl.loop(0, tiles)
     def _(turn):
-        home = (me_ref[0] - turn + tiles) % tiles * share
-        for group in range(groups):
-            rows_ref, cols_ref = rows_refs[group], cols_refs[group]
-            at = pl.ds(pl.multiple_of(home + group * size, size), size)
-            for piece in range(rows_ref.shape[0]):
-                place = pl.multiple_of(home + piece * columns + group * size, size)
-                for comp in range(6):
-                    staged[comp, pl.ds(place, size), :] = rows_ref[piece, turn, 0, comp]
-            part = lambda where, comp: cols_ref[turn, where + PER_PLANE, comp]
-            for disp in range(disps):
-                for heading in range(6):
-                    @pl.when(dirs_ref[disp] == heading)
-                    def _(disp=disp, heading=heading):
-                        spatial = heading % 3
-                        step = 1 if heading < 3 else -1
-                        source = moved(part, chunk, spatial, step, chunk + step * PER_PLANE)
-                        table = links_ref if step > 0 else back_ref
-                        total = apply_link(table, chunk, spatial, step < 0, source, [None] * 6)
-                        for comp in range(6):
-                            shifted[disp, comp, at, :] = total[comp]
+        home = (me_ref[0] - turn + tiles) % tiles * size
+        for piece in range(rows_ref.shape[0]):
+            place = pl.multiple_of(home + piece * columns, size)
+            for comp in range(6):
+                staged[comp, pl.ds(place, size), :] = rows_ref[piece, turn, 0, comp]
 
     for colour in range(3):
         real_at = pl.ds(2 * colour * LANES, LANES)
@@ -243,8 +252,7 @@
     norm = 1.0 / math.sqrt(3.0 * sites * tiles)
     me = lax.axis_index("tile")
     here = me.reshape(1).astype(jnp.int32)
-    size = 8 if share % 8 == 0 else share
-    groups = share // size
+    groups, size = 1, share
 
     def passed(value, steps):
         if steps % tiles == 0:
@@ -252,7 +260,13 @@
         return lax.ppermute(value, "tile", [(i, (i + steps) % tiles) for i in range(tiles)])
 
     own_links = links.reshape(3, 18, chunks, LANES).transpose(2, 0, 1, 3)
-    all_links = lax.all_gather(own_links, "tile", axis=0, tiled=True)
+    quarters = math.gcd(lax.axis_size("vec"), chunks)
+    some_chunks = chunks // quarters
+    mine_at = lax.axis_index("vec") % quarters * some_chunks
+    quarter = lax.dynamic_slice_in_dim(own_links, mine_at, some_chunks, 0)
+    quarter = lax.all_gather(quarter, "tile", axis=0)
+    all_links = lax.all_gather(quarter, "vec", axis=0)[:quarters]
+    all_links = all_links.transpose(1, 0, 2, 3, 4, 5).reshape(every, 3, 18, LANES)
     field = vectors.reshape(2, tiles, groups, size, 3, chunks, LANES)
     field = field.transpose(2, 1, 5, 0, 4, 3, 6)
     field = field.reshape(groups, tiles, chunks, 6, size, LANES)
@@ -311,21 +325,31 @@
     row_block = pl.BlockSpec(
         (row_count // nv, tiles, 1, 6, size, LANES), lambda i: (0, 0, i, 0, 0, 0)
     )
+    displaced = pl.pallas_call(
+        displace_kernel,
+        out_shape=jax.ShapeDtypeStruct((chunks, disps, 6, nv, LANES), jnp.float32),
+        in_specs=[smem, smem, vmem, vmem, vmem],
+        out_specs=vmem,
+        compiler_params=pltpu.CompilerParams(vmem_limit_bytes=VMEM_LIMIT),
+        name="displace",
+    )(here, directions, wide[0], own_links, own_back)
     parts = []
     for half in range(halves):
         pick = slice(half * some, (half + 1) * some)
         partial = pl.pallas_call(
-            functools.partial(contract_kernel, groups),
+            contract_kernel,
             grid=(chunks,),
             out_shape=jax.ShapeDtypeStruct((2 * row_count, width), jnp.float32),
-            in_specs=[smem, smem]
-            + [row_block] * groups
-            + [vmem] * groups
-            + [vmem, vmem, one((some, LANES)), one((some, LANES))],
+            in_specs=[
+                smem,
+                row_block,
+                one((disps, 6, nv, LANES)),
+                one((some, LANES)),
+                one((some, LANES)),
+            ],
             out_specs=pl.BlockSpec((2 * row_count, width), lambda i: (0, 0)),
             scratch_shapes=[
                 pltpu.VMEM((6, row_count, LANES), jnp.float32),
-                pltpu.VMEM((disps, 6, nv, LANES), jnp.float32),
                 pltpu.VMEM((2 * row_count, depth), jnp.bfloat16),
                 pltpu.VMEM((2 * row_count, depth), jnp.bfloat16),
                 pltpu.VMEM((width, depth), jnp.bfloat16),
@@ -336,7 +360,7 @@
                 flops=20 * 10**9, bytes_accessed=12 * 10**6, transcendentals=0
             ),
             name="contract",
-        )(here, directions, *gathered, *wide, own_links, own_back, cosine[:, pick], sine[:, pick])
+        )(here, gathered[0], displaced, cosine[:, pick], sine[:, pick])
         partial = partial.reshape(2, row_count, width)
         mine = lax.psum_scatter(partial, "tile", scatter_dimension=1, tiled=True)
         parts.append(mine.reshape(2, row_count // tiles, some, disps, nv))

time: 300 us -> 270 us (0.900)
  Pallas kernels: 110 us -> 76.5 us
  blocking collectives: 33.3 us -> 52 us
  starting transfers between devices: 28.3 us -> 18.5 us
  waiting for transfers between devices: 95.2 us -> 92 us
    pallas_call x2 -> x3, Pallas kernels: 68.6 us -> 48.9 us  [the longest x2 42.3 us: local(): pl.pallas_call(contract_kernel, grid=(chunks,), out_shape=jax.ShapeDtypeS...]
    all_gather x1 -> x2, blocking collectives: 33.3 us -> 52 us  [the longest x1 42.9 us: local(): quarter = lax.all_gather(quarter, 'tile', axis=0)]
    pallas_call x2 -> x1, Pallas kernels: 41.8 us -> 27.6 us  [local(): *done, own_back = run_filter(here, *ordered, all_links)]
    ppermute x16 -> x8, starting transfers between devices: 28.1 us -> 18.4 us  [passed(): lax.ppermute(value, 'tile', [(i, (i + steps) % tiles) for i in range(tile...]
    ppermute x16 -> x8, waiting for transfers between devices: 67.4 us -> 58.7 us  [passed(): lax.ppermute(value, 'tile', [(i, (i + steps) % tiles) for i in range(tile...]
    reduce_scatter x2, waiting for transfers between devices: 27.7 us -> 33.3 us  [local(): mine = lax.psum_scatter(partial, 'tile', scatter_dimension=1, tiled=True)]
  transfers between devices with their start and end apart: 20 -> 11, of which waited for: 11 -> 6; matrix products, arithmetic and copies ran while one was open for 4% -> 3% of each run, Pallas kernels for 18% -> 10%
where the time goes in v3:
time: 270 us
  waiting for transfers between devices  92 us (34%)
  Pallas kernels  76.5 us (28%)
  blocking collectives  52 us (19%)
  starting transfers between devices  18.5 us (7%)
  between operations  13.3 us (5%)
  local copies, waits for them, and re-layouts  12.4 us (5%)
  other arithmetic  4.97 us (2%)
    ppermute x8, waiting for transfers between devices, passed(): lax.ppermute(value, 'tile', [(i, (i + steps) % tiles) for i in range(tile...  58.7 us
    all_gather x1, blocking collectives, local(): quarter = lax.all_gather(quarter, 'tile', axis=0)  42.9 us
    pallas_call x2, Pallas kernels, local(): pl.pallas_call(contract_kernel, grid=(chunks,), out_shape=jax.ShapeDtypeS...  42.3 us
    reduce_scatter x2, waiting for transfers between devices, local(): mine = lax.psum_scatter(partial, 'tile', scatter_dimension=1, tiled=True)  33.3 us
    pallas_call x1, Pallas kernels, local(): *done, own_back = run_filter(here, *ordered, all_links)  27.6 us
    ppermute x8, starting transfers between devices, passed(): lax.ppermute(value, 'tile', [(i, (i + steps) % tiles) for i in range(tile...  18.4 us
    all_gather x1, blocking collectives, local(): all_links = lax.all_gather(quarter, 'vec', axis=0)[:quarters]  9.13 us
    pallas_call x1, Pallas kernels, local(): pl.pallas_call(displace_kernel, out_shape=jax.ShapeDtypeStruct((chunks, d...  6.61 us
  transfers between devices with their start and end apart: 11, of which 6 were waited for; matrix products, arithmetic and copies ran while one was open for 3% of the time, Pallas kernels for 10%

profile of v3, /device:TPU:0, one launch (start us, length us, event | category | flops | bytes accessed | tf_op | source)
XLA Modules:
  0.0 269.7 jit_solution(7358122638417595032)
XLA Ops:
  6.5 1.7 copy.25
  8.6 0.9 dynamic-slice_bitcast_fusion
  9.5 5.1 %collective-permute-start = (f32[8,6,16,128]{3,2,1,0:T(8,128)S(1)}, f32[8,6,16,128]{3,2,1,0:T(8,128)S(1)}, u32[]{:S(2)}, u32[]{:S(2)}) collective-permute-start(f32[8,6,16,128]{3,2,1,0:T(8,128)S(1)} %get-tuple-element.19), channel_id=1, source_target_pairs={{0,12},{4,0},{8,4},{12,8},{1,13},{5,1},{9,5},{13,9},{2,14},{6,2},{... | collective-permute-start | bytes 1179656 | tf_op jit(solution)/shard_map/ppermute | solution.py:260
  14.6 1.0 collective-permute-start.2
  15.9 42.9 %all-gather = f32[8,3,18,128]{3,2,1,0:T(8,128)S(1)} all-gather(f32[2,3,18,128]{3,2,1,0:T(8,128)S(1)} %copy.19), channel_id=2, replica_groups=mesh['groups'=2,'tile'=4,'vec'=4] {'tile'}, dimensions={0}, use_global_device_ids=true | all-gather | bytes 276480 | tf_op jit(solution)/shard_map/all_gather | solution.py:267
  58.9 9.1 %all-gather.1 = f32[16,2,3,18,128]{4,1,3,2,0:T(2,128)S(1)} all-gather(f32[4,2,3,18,128]{4,1,3,2,0:T(2,128)S(1)} %copy.20), channel_id=3, replica_groups=mesh['groups'=2,'tile'=4,'vec'=4] {'vec'}, dimensions={0}, use_global_device_ids=true | all-gather | bytes 1105920 | tf_op jit(solution)/shard_map/all_gather | solution.py:268
  68.1 1.3 copy.22
  70.5 27.6 %filter.1 = (f32[8,6,16,128]{3,2,1,0:T(8,128)}, f32[8,6,16,128]{3,2,1,0:T(8,128)}, f32[8,6,16,128]{3,2,1,0:T(8,128)}, f32[8,6,16,128]{3,2,1,0:T(8,128)}, f32[8,3,18,128]{3,2,1,0:T(8,128)}) custom-call(s32[1]{0:T(128)} %bitcast.me_ref, f32[8,6,16,128]{3,2,1,0:T(8,128)} %get-tuple-element.20.refs_0_, f32[8,6,16,128]{3,2,1,0:T(8,128)} %copy-done.4, ...), custom_call_target="tpu_custom_call" | custom-call | flops 12000000000 | bytes 2000000 | tf_op jit(solution)/shard_map/filter/pallas_call | solution.py:300
  98.8 3.1 %collective-permute-start.5 = (f32[8,6,16,128]{3,2,1,0:T(8,128)}, f32[8,6,16,128]{3,2,1,0:T(8,128)S(1)}, u32[]{:S(2)}, u32[]{:S(2)}) collective-permute-start(f32[8,6,16,128]{3,2,1,0:T(8,128)} %get-tuple-element.13), channel_id=1, source_target_pairs={{0,12},{4,0},{8,4},{12,8},{1,13},{5,1},{9,5},{13,9},{2,14},{6,2},{... | collective-permute-start | bytes 1179656 | tf_op jit(solution)/shard_map/ppermute | solution.py:260
  101.9 10.3 %collective-permute-done.3 = f32[8,6,16,128]{3,2,1,0:T(8,128)S(1)} collective-permute-done((f32[8,6,16,128]{3,2,1,0:T(8,128)}, f32[8,6,16,128]{3,2,1,0:T(8,128)S(1)}, u32[]{:S(2)}, u32[]{:S(2)}) %collective-permute-start.3) | collective-permute-done | bytes 393248 | tf_op jit(solution)/shard_map/ppermute | solution.py:260
  112.2 15.9 %collective-permute-done.4 = f32[8,6,16,128]{3,2,1,0:T(8,128)S(1)} collective-permute-done((f32[8,6,16,128]{3,2,1,0:T(8,128)}, f32[8,6,16,128]{3,2,1,0:T(8,128)S(1)}, u32[]{:S(2)}, u32[]{:S(2)}) %collective-permute-start.4) | collective-permute-done | bytes 393248 | tf_op jit(solution)/shard_map/ppermute | solution.py:260
  128.1 2.3 pad_maximum_fusion
  132.1 8.4 %collective-permute-start.6 = (f32[4,4,6,16,128]{4,3,2,1,0:T(8,128)S(1)}, f32[4,4,6,16,128]{4,3,2,1,0:T(8,128)S(1)}, u32[]{:S(2)}, u32[]{:S(2)}) collective-permute-start(f32[4,4,6,16,128]{4,3,2,1,0:T(8,128)S(1)} %get-tuple-element.15), channel_id=1, source_target_pairs={{0,4},{4,8},{8,12},{12,0},{1,5},{5,9},{9,13},{13,1},{2,6},{6,10},{... | collective-permute-start | bytes 2359304 | tf_op jit(solution)/shard_map/ppermute | solution.py:260
  142.1 16.9 %collective-permute-done.6 = f32[4,4,6,16,128]{4,3,2,1,0:T(8,128)S(1)} collective-permute-done((f32[4,4,6,16,128]{4,3,2,1,0:T(8,128)S(1)}, f32[4,4,6,16,128]{4,3,2,1,0:T(8,128)S(1)}, u32[]{:S(2)}, u32[]{:S(2)}) %collective-permute-start.6) | collective-permute-done | bytes 786464 | tf_op jit(solution)/shard_map/ppermute | solution.py:260
  159.0 15.6 %collective-permute-done.7 = f32[4,4,6,16,128]{4,3,2,1,0:T(8,128)S(1)} collective-permute-done((f32[4,4,6,16,128]{4,3,2,1,0:T(8,128)S(1)}, f32[4,4,6,16,128]{4,3,2,1,0:T(8,128)S(1)}, u32[]{:S(2)}, u32[]{:S(2)}) %collective-permute-start.7) | collective-permute-done | bytes 786464 | tf_op jit(solution)/shard_map/ppermute | solution.py:260
  174.7 1.8 maximum_maximum_fusion.cols_ref
  176.5 6.6 %displace.1.shifted_ref = f32[8,2,6,64,128]{4,3,2,1,0:T(8,128)} custom-call(s32[1]{0:T(128)} %bitcast.me_ref, s32[2]{0:T(128)} %dirs_ref.1, f32[4,16,6,16,128]{4,3,2,1,0:T(8,128)} %maximum_maximum_fusion.cols_ref, f32[8,3,18,128]{3,2,1,0:T(8,128)} %bitcast.56, f32[8,3,18,128]{3,2,1,0:T(8,128)} %get-tuple-element.14.back_ref), custom_call_target="tpu_custom_call" | custom-call | tf_op jit(solution)/shard_map/displace/pallas_call | solution.py:328
  183.1 21.2 %contract.2 = f32[512,512]{1,0:T(8,128)} custom-call(s32[1]{0:T(128)} %bitcast.me_ref, f32[4,4,8,6,16,128]{5,4,3,2,1,0:T(8,128)} %bitcast.61, f32[8,2,6,64,128]{4,3,2,1,0:T(8,128)} %displace.1.shifted_ref, f32[8,4,128]{2,1,0:T(4,128)} %get-tuple-element.23.cos_ref, f32[8,4,128]{2,1,0:T(4,128)} %get-tuple-element.21.sin_ref), custom_call_target="tpu_custom_call" | custom-call | flops 20000000000 | bytes 12000000 | tf_op jit(solution)/shard_map/contract/pallas_call | solution.py:339
  204.3 21.2 %contract.3 = f32[512,512]{1,0:T(8,128)} custom-call(s32[1]{0:T(128)} %bitcast.me_ref, f32[4,4,8,6,16,128]{5,4,3,2,1,0:T(8,128)} %bitcast.62, f32[8,2,6,64,128]{4,3,2,1,0:T(8,128)} %displace.1.shifted_ref, f32[8,4,128]{2,1,0:T(4,128)} %get-tuple-element.24.cos_ref, f32[8,4,128]{2,1,0:T(4,128)} %get-tuple-element.22.sin_ref), custom_call_target="tpu_custom_call" | custom-call | flops 20000000000 | bytes 12000000 | tf_op jit(solution)/shard_map/contract/pallas_call | solution.py:339
  225.5 6.5 %reduce-scatter.3.cloned.1.call-done = f32[2,64,512]{2,1,0:T(8,128)} async-done(((f32[2,256,512]{2,1,0:T(8,128)}), f32[2,64,512]{2,1,0:T(8,128)}) %reduce-scatter.3.cloned.1.call-update) | async-done | bytes 262160 | tf_op jit(solution)/shard_map/reduce_scatter | solution.py:365
  232.0 1.3 reshape.159
  233.4 26.8 %reduce-scatter.5.cloned.1.call-done = f32[2,64,512]{2,1,0:T(8,128)} async-done(((f32[2,256,512]{2,1,0:T(8,128)}), f32[2,64,512]{2,1,0:T(8,128)}) %reduce-scatter.5.cloned.1.call-update) | async-done | bytes 262160 | tf_op jit(solution)/shard_map/reduce_scatter | solution.py:365
  260.2 1.3 reshape.161
  262.0 1.1 copy.24
  (49 shorter events, 6.4 us)
Async XLA Ops:
  6.5 176.6 %all-gather.5.cloned.1.call-start = ((), (), s32[]{:S(2)}) async-start(), calls=%async_computation.4 | async-start | bytes 7864320 | tf_op jit(solution)/shard_map/all_gather | solution.py:303
  8.3 7.3 %copy-start.2 = (f32[3,2,3,3,1024]{4,1,3,2,0:T(2,128)S(1)}, f32[3,2,3,3,1024]{4,1,3,2,0:T(2,128)}, u32[]{:S(2)}) copy-start(f32[3,2,3,3,1024]{4,1,3,2,0:T(2,128)} %param.5) | copy-start | bytes 663556
  9.5 60.0 %collective-permute-start = (f32[8,6,16,128]{3,2,1,0:T(8,128)S(1)}, f32[8,6,16,128]{3,2,1,0:T(8,128)S(1)}, u32[]{:S(2)}, u32[]{:S(2)}) collective-permute-start(f32[8,6,16,128]{3,2,1,0:T(8,128)S(1)} %get-tuple-element.19), channel_id=1, source_target_pairs={{0,12},{4,0},{8,4},{12,8},{1,13},{5,1},{9,5},{13,9},{2,14},{6,2},{... | collective-permute-start | bytes 1179656 | tf_op jit(solution)/shard_map/ppermute | solution.py:260
  14.6 54.9 %collective-permute-start.1 = (f32[8,6,16,128]{3,2,1,0:T(8,128)S(1)}, f32[8,6,16,128]{3,2,1,0:T(8,128)S(1)}, u32[]{:S(2)}, u32[]{:S(2)}) collective-permute-start(f32[8,6,16,128]{3,2,1,0:T(8,128)S(1)} %get-tuple-element.18), channel_id=1, source_target_pairs={{0,8},{4,12},{8,0},{12,4},{1,9},{5,13},{9,1},{13,5},{2,10},{6,14},... | collective-permute-start | bytes 1179656 | tf_op jit(solution)/shard_map/ppermute | solution.py:260
  14.6 54.9 %collective-permute-start.2 = (f32[8,6,16,128]{3,2,1,0:T(8,128)S(1)}, f32[8,6,16,128]{3,2,1,0:T(8,128)S(1)}, u32[]{:S(2)}, u32[]{:S(2)}) collective-permute-start(f32[8,6,16,128]{3,2,1,0:T(8,128)S(1)} %get-tuple-element.17), channel_id=1, source_target_pairs={{0,4},{4,8},{8,12},{12,0},{1,5},{5,9},{9,13},{13,1},{2,6},{6,10},{... | collective-permute-start | bytes 1179656 | tf_op jit(solution)/shard_map/ppermute | solution.py:260
  69.4 0.8 copy-start.4
  69.5 0.9 copy-start.5
  69.5 1.0 copy-start.6
  98.0 33.2 %copy-start.3 = (s32[8,3]{0,1:T(4,128)S(1)}, s32[8,3]{0,1:T(4,128)}, u32[]{:S(2)}) copy-start(s32[8,3]{0,1:T(4,128)} %param.6) | copy-start | bytes 292
  98.0 14.1 %collective-permute-start.3 = (f32[8,6,16,128]{3,2,1,0:T(8,128)}, f32[8,6,16,128]{3,2,1,0:T(8,128)S(1)}, u32[]{:S(2)}, u32[]{:S(2)}) collective-permute-start(f32[8,6,16,128]{3,2,1,0:T(8,128)} %get-tuple-element.11), channel_id=1, source_target_pairs={{0,4},{4,8},{8,12},{12,0},{1,5},{5,9},{9,13},{13,1},{2,6},{6,10},{... | collective-permute-start | bytes 1179656 | tf_op jit(solution)/shard_map/ppermute | solution.py:260
  98.0 30.1 %collective-permute-start.4 = (f32[8,6,16,128]{3,2,1,0:T(8,128)}, f32[8,6,16,128]{3,2,1,0:T(8,128)S(1)}, u32[]{:S(2)}, u32[]{:S(2)}) collective-permute-start(f32[8,6,16,128]{3,2,1,0:T(8,128)} %get-tuple-element.12), channel_id=1, source_target_pairs={{0,8},{4,12},{8,0},{12,4},{1,9},{5,13},{9,1},{13,5},{2,10},{6,14},... | collective-permute-start | bytes 1179656 | tf_op jit(solution)/shard_map/ppermute | solution.py:260
  98.8 29.3 %collective-permute-start.5 = (f32[8,6,16,128]{3,2,1,0:T(8,128)}, f32[8,6,16,128]{3,2,1,0:T(8,128)S(1)}, u32[]{:S(2)}, u32[]{:S(2)}) collective-permute-start(f32[8,6,16,128]{3,2,1,0:T(8,128)} %get-tuple-element.13), channel_id=1, source_target_pairs={{0,12},{4,0},{8,4},{12,8},{1,13},{5,1},{9,5},{13,9},{2,14},{6,2},{... | collective-permute-start | bytes 1179656 | tf_op jit(solution)/shard_map/ppermute | solution.py:260
  130.4 1.5 copy-start
  130.4 101.6 %reduce-scatter.3.cloned.1.call-start = ((), (), s32[]{:S(2)}) async-start(), calls=%async_computation.2 | async-start | bytes 1310720 | tf_op jit(solution)/shard_map/reduce_scatter | solution.py:365
  131.9 42.7 %copy-start.1 = (f32[8,6,16,128]{3,2,1,0:T(8,128)S(1)}, f32[8,6,16,128]{3,2,1,0:T(8,128)}, u32[]{:S(2)}) copy-start(f32[8,6,16,128]{3,2,1,0:T(8,128)} %get-tuple-element.10) | copy-start | bytes 1179652
  132.1 26.8 %collective-permute-start.6 = (f32[4,4,6,16,128]{4,3,2,1,0:T(8,128)S(1)}, f32[4,4,6,16,128]{4,3,2,1,0:T(8,128)S(1)}, u32[]{:S(2)}, u32[]{:S(2)}) collective-permute-start(f32[4,4,6,16,128]{4,3,2,1,0:T(8,128)S(1)} %get-tuple-element.15), channel_id=1, source_target_pairs={{0,4},{4,8},{8,12},{12,0},{1,5},{5,9},{9,13},{13,1},{2,6},{6,10},{... | collective-permute-start | bytes 2359304 | tf_op jit(solution)/shard_map/ppermute | solution.py:260
  140.5 34.1 %collective-permute-start.7 = (f32[4,4,6,16,128]{4,3,2,1,0:T(8,128)S(1)}, f32[4,4,6,16,128]{4,3,2,1,0:T(8,128)S(1)}, u32[]{:S(2)}, u32[]{:S(2)}) collective-permute-start(f32[4,4,6,16,128]{4,3,2,1,0:T(8,128)S(1)} %get-tuple-element.16), channel_id=1, source_target_pairs={{0,12},{4,0},{8,4},{12,8},{1,13},{5,1},{9,5},{13,9},{2,14},{6,2},{... | collective-permute-start | bytes 2359304 | tf_op jit(solution)/shard_map/ppermute | solution.py:260
  204.3 55.9 %reduce-scatter.5.cloned.1.call-start = ((), (), s32[]{:S(2)}) async-start(), calls=%async_computation.3 | async-start | bytes 1310720 | tf_op jit(solution)/shard_map/reduce_scatter | solution.py:365
Sparse Core Ops, SparseCore 0:
  130.6 51.4 all-gather.4
  204.4 27.5 reduce-scatter.2
  234.3 25.7 reduce-scatter.4
